TPU v7x, 32 devices: a whole 2x2x4 slice. The times are simulated.
32 devices in a mesh: fsdp: 8 (over y, x, core), tp: 4 (over z).
Axes of the slice: x: 2, y: 2, z: 4, core: 2. Of those that a mesh axis runs over, the one named last changes fastest.
Arguments:
- hidden_in: bfloat16 [8192, 2048], P(('fsdp', 'tp')), may hold values from -6 to 6
- seq_lengths: int32 [8], P('fsdp'), may hold values from 512 to 1024, as said below
- seq_offsets: int32 [8], P('fsdp'), may hold values from 0 to 512, as said below
- routes: int32 [8192, 8], P(('fsdp', 'tp')), may hold values from 0 to 15, all different within a row; in each aligned block of 256 rows (0 to 255, 256 to 511, ...) at most 144 rows name the same one
- attn_gain: float32 [2048], P('fsdp'), may hold values from 0.5 to 1.5
- w_query: float32 [2048, 2048], P('fsdp', 'tp'), may hold values from -0.125 to 0.125
- w_key: float32 [2048, 2048], P('fsdp', 'tp'), may hold values from -0.125 to 0.125
- w_value: float32 [2048, 2048], P('fsdp', 'tp'), may hold values from -0.125 to 0.125
- query_gain: float32 [128], P('fsdp'), may hold values from 0.5 to 1.5
- key_gain: float32 [128], P('fsdp'), may hold values from 0.5 to 1.5
- w_output: float32 [2048, 2048], P('tp', 'fsdp'), may hold values from -2 to 2
- ffn_gain: float32 [2048], P('fsdp'), may hold values from 0.5 to 1.5
- router: float32 [2048, 16], P('fsdp'), may hold values from -0.0625 to 0.0625
- w_gate: float32 [16, 2048, 1024], P('fsdp', None, 'tp'), may hold values from -0.125 to 0.125
- w_up: float32 [16, 2048, 1024], P('fsdp', None, 'tp'), may hold values from -0.125 to 0.125
- w_down: float32 [16, 1024, 2048], P('fsdp', 'tp'), may hold values from -2 to 2
- cotangent: float32 [8192, 2048], P(('fsdp', 'tp')), may hold values from -6 to 6
Outputs:
- block_out: bfloat16 [8192, 2048], P(('fsdp', 'tp'))
- grad_input: float32 [8192, 2048], P(('fsdp', 'tp'))
- grad_attn_gain: float32 [2048], P(('fsdp', 'tp'))
- grad_w_query: float32 [2048, 2048], P('fsdp', 'tp')
- grad_w_key: float32 [2048, 2048], P('fsdp', 'tp')
- grad_w_value: float32 [2048, 2048], P('fsdp', 'tp')
- grad_query_gain: float32 [128], P(('fsdp', 'tp'))
- grad_key_gain: float32 [128], P(('fsdp', 'tp'))
- grad_w_output: float32 [2048, 2048], P('tp', 'fsdp')
- grad_ffn_gain: float32 [2048], P(('fsdp', 'tp'))
- grad_router: float32 [2048, 16], P(('fsdp', 'tp'))
- grad_w_gate: float32 [16, 2048, 1024], P('fsdp', None, 'tp')
- grad_w_up: float32 [16, 2048, 1024], P('fsdp', None, 'tp')
- grad_w_down: float32 [16, 1024, 2048], P('fsdp', 'tp')
Inputs may be any that keep to these rules, and one draw needn't show every extreme that they name: `seq_lengths`: real tokens of the sequence in each slot of 1024 rows; some slot is full and some slot is half full. `seq_offsets`: row within its slot at which each sequence starts; offset plus length is at most 1024. `routes`: each row names 8 different experts; among the rows of one device no expert is named more than 144 times, a bound that some block reaches.
All inputs are finite; a program needn't handle non-finite values.
Results may differ from a plain program's by a relative error of at most 0.025.
Values may be sent and summed in bfloat16 or wider, within the bound.
No kernel may reach another device: no remote copies, remote signals or barrier semaphores. Data moves between devices by JAX's collectives and lax.ppermute only.
A program may use at most 320 MiB of HBM per device.

v0:
```python
import functools

import jax
import jax.numpy as jnp
from jax import lax
from jax.sharding import PartitionSpec as P

HD = 128


NORM_EPSILON = 1e-06
ROPE_THETA = 10000.0


def rms_norm(values, gain_vec):
    return (
        values
        * lax.rsqrt(jnp.mean(values * values, axis=-1, keepdims=True) + NORM_EPSILON)
        * gain_vec
    )


def rotary_tables(positions, width):
    half_width = width // 2
    frequency = ROPE_THETA ** (-(jnp.arange(half_width, dtype=jnp.float32) * 2.0 / width))
    angles = positions.astype(jnp.float32)[:, None] * frequency[None, :]
    angles = jnp.concatenate([angles, angles], axis=1)
    return (jnp.cos(angles), jnp.sin(angles))


def head_prepare(pre_values, gain_vec, cos_table, sin_table):
    seq_rows = pre_values.shape[0]
    shaped = pre_values.reshape(seq_rows, -1, gain_vec.shape[0])
    normed = rms_norm(shaped, gain_vec)
    half_width = gain_vec.shape[0] // 2
    rotated = jnp.concatenate([-normed[..., half_width:], normed[..., :half_width]], axis=-1)
    turned = normed * cos_table[:, None, :] + rotated * sin_table[:, None, :]
    return turned.reshape(pre_values.shape)


def swiglu(gate_val, up_val):
    return jax.nn.silu(gate_val) * up_val


def gate_pick(logits, one_hot):
    return jnp.sum(jax.nn.softmax(logits, axis=-1)[:, None, :] * one_hot, axis=-1)


def whole_group(values):
    return lax.all_gather(values, "tp", axis=0, tiled=True)


def head_sum(term_fn, rows_local):
    return lax.psum_scatter(
        term_fn(jnp.int32(0), lax.axis_size("tp") * rows_local).astype(jnp.bfloat16),
        "tp",
        scatter_dimension=0,
        tiled=True,
    ).astype(jnp.float32)


def to_experts(buffer):
    return lax.all_to_all(buffer, "fsdp", split_axis=0, concat_axis=0, tiled=True)


def from_experts(buffer):
    return lax.all_to_all(buffer, "fsdp", split_axis=0, concat_axis=0, tiled=True)


def per_device(
    hidden_in,
    seq_lengths,
    seq_offsets,
    routes,
    attn_gain,
    w_query,
    w_key,
    w_value,
    query_gain,
    key_gain,
    w_output,
    ffn_gain,
    router,
    w_gate,
    w_up,
    w_down,
    cotangent,
):
    tp_size = lax.axis_size("tp")
    rows_local = hidden_in.shape[0]
    model_width = hidden_in.shape[1]
    group_rows = rows_local * tp_size
    top_count = routes.shape[1]
    experts = router.shape[1]
    expert_local = w_gate.shape[0]
    fsdp_count = experts // expert_local
    capacity = 9 * rows_local * top_count // (8 * experts)
    heads_local = w_output.shape[0] // HD
    block_rows = min(512, group_rows)
    block_count = group_rows // block_rows
    score_scale = HD ** (-0.5)
    row_first = lax.axis_index("tp") * rows_local
    seq_start = seq_offsets[0]
    seq_end = seq_start + seq_lengths[0]
    group_place = jnp.arange(group_rows, dtype=jnp.int32)
    key_valid = (group_place >= seq_start) & (group_place < seq_end)
    local_place = row_first + jnp.arange(rows_local, dtype=jnp.int32)
    row_keep = ((local_place >= seq_start) & (local_place < seq_end)).astype(jnp.float32)[:, None]
    cos_table, sin_table = rotary_tables(group_place - seq_start, HD)
    (
        gain_attn,
        gain_query,
        gain_key,
        gain_ffn,
        router_full,
        query_full,
        key_full,
        value_full,
        output_full,
    ) = (
        lax.all_gather(attn_gain.astype(jnp.bfloat16), "fsdp", axis=0, tiled=True),
        lax.all_gather(query_gain.astype(jnp.bfloat16), "fsdp", axis=0, tiled=True),
        lax.all_gather(key_gain.astype(jnp.bfloat16), "fsdp", axis=0, tiled=True),
        lax.all_gather(ffn_gain.astype(jnp.bfloat16), "fsdp", axis=0, tiled=True),
        lax.all_gather(router.astype(jnp.bfloat16), "fsdp", axis=0, tiled=True),
        lax.all_gather(w_query.astype(jnp.bfloat16), "fsdp", axis=0, tiled=True),
        lax.all_gather(w_key.astype(jnp.bfloat16), "fsdp", axis=0, tiled=True),
        lax.all_gather(w_value.astype(jnp.bfloat16), "fsdp", axis=0, tiled=True),
        lax.all_gather(w_output.astype(jnp.bfloat16), "fsdp", axis=1, tiled=True),
    )
    residual_in = hidden_in.astype(jnp.float32)
    attn_gain_f = gain_attn.astype(jnp.float32)
    normed = rms_norm(residual_in, attn_gain_f).astype(jnp.bfloat16)
    group_normed = whole_group(normed)
    query_pre = jnp.dot(group_normed, query_full, preferred_element_type=jnp.float32)
    key_pre = jnp.dot(group_normed, key_full, preferred_element_type=jnp.float32)
    value_low = jnp.dot(group_normed, value_full, preferred_element_type=jnp.float32).astype(
        jnp.bfloat16
    )
    query_gain_f = gain_query.astype(jnp.float32)
    key_gain_f = gain_key.astype(jnp.float32)
    query_low = head_prepare(query_pre, query_gain_f, cos_table, sin_table).astype(jnp.bfloat16)
    key_low = head_prepare(key_pre, key_gain_f, cos_table, sin_table).astype(jnp.bfloat16)
    key_heads = key_low.reshape(group_rows, heads_local, HD)
    value_heads = value_low.reshape(group_rows, heads_local, HD)
    query_blocks = query_low.reshape(block_count, block_rows, heads_local, HD)

    def forward_block(query_block):
        scores = (
            jnp.einsum("qhd,khd->hqk", query_block, key_heads, preferred_element_type=jnp.float32)
            * score_scale
        )
        scores = jnp.where(key_valid[None, None, :], scores, -1e30)
        row_max = jnp.max(scores, axis=-1, keepdims=True)
        exp_scores = jnp.exp(scores - row_max)
        row_total = jnp.sum(exp_scores, axis=-1, keepdims=True)
        attn_prob = (exp_scores / row_total).astype(jnp.bfloat16)
        mixed_block = jnp.einsum(
            "hqk,khd->qhd", attn_prob, value_heads, preferred_element_type=jnp.float32
        )
        return (mixed_block.astype(jnp.bfloat16), (row_max + jnp.log(row_total))[..., 0])

    mixed_blocks, log_totals = lax.map(forward_block, query_blocks)
    mixed_out = mixed_blocks.reshape(group_rows, heads_local * HD)

    def attn_term(row_start, row_count):
        return jnp.dot(mixed_out, output_full, preferred_element_type=jnp.float32)

    attn_out = head_sum(attn_term, rows_local)
    residual = residual_in + row_keep * attn_out
    ffn_gain_f = gain_ffn.astype(jnp.float32)
    ffn_normed = rms_norm(residual, ffn_gain_f).astype(jnp.bfloat16)
    logits = jnp.dot(ffn_normed, router_full, preferred_element_type=jnp.float32)
    one_hot_routes = (
        routes[:, :, None] == jnp.arange(experts, dtype=jnp.int32)[None, None, :]
    ).astype(jnp.float32)
    gate_weights = gate_pick(logits, one_hot_routes)
    expert_of = routes.reshape(-1)
    assign_count = rows_local * top_count
    assign_hot = (expert_of[:, None] == jnp.arange(experts, dtype=jnp.int32)[None, :]).astype(
        jnp.int32
    )
    slot_rank = jnp.sum((jnp.cumsum(assign_hot, axis=0) - 1) * assign_hot, axis=1)
    slot_place = expert_of * capacity + slot_rank
    slot_owner = (
        jnp.full((experts * capacity,), assign_count, jnp.int32)
        .at[slot_place]
        .set(jnp.arange(assign_count, dtype=jnp.int32))
    )
    padded = jnp.concatenate([ffn_normed, jnp.zeros((1, model_width), jnp.bfloat16)], axis=0)
    sent_rows = padded[slot_owner // top_count].reshape(
        fsdp_count, expert_local, capacity, model_width
    )
    arrived = to_experts(sent_rows)
    gate_local = w_gate.astype(jnp.bfloat16)
    up_local = w_up.astype(jnp.bfloat16)
    down_local = w_down.astype(jnp.bfloat16)
    gate_full, up_full, down_full = (
        lax.all_gather(gate_local, "tp", axis=2, tiled=True),
        lax.all_gather(up_local, "tp", axis=2, tiled=True),
        lax.all_gather(down_local, "tp", axis=1, tiled=True),
    )
    gate_val = jnp.einsum("secd,edf->secf", arrived, gate_full, preferred_element_type=jnp.float32)
    up_val = jnp.einsum("secd,edf->secf", arrived, up_full, preferred_element_type=jnp.float32)
    hidden = swiglu(gate_val, up_val).astype(jnp.bfloat16)
    expert_out = jnp.einsum(
        "secf,efd->secd", hidden, down_full, preferred_element_type=jnp.float32
    ).astype(jnp.bfloat16)
    returned = from_experts(expert_out).reshape(experts * capacity, model_width)
    out_rows = returned[slot_place].reshape(rows_local, top_count, model_width).astype(jnp.float32)
    mixture = jnp.sum(gate_weights[:, :, None] * out_rows, axis=1)
    block_out = (residual + row_keep * mixture).astype(jnp.bfloat16)
    grad_mixture = row_keep * cotangent
    grad_gates = jnp.sum(grad_mixture[:, None, :] * out_rows, axis=-1)
    grad_slots = (
        (gate_weights[:, :, None] * grad_mixture[:, None, :])
        .astype(jnp.bfloat16)
        .reshape(assign_count, model_width)
    )
    grad_padded = jnp.concatenate([grad_slots, jnp.zeros((1, model_width), jnp.bfloat16)], axis=0)
    grad_sent = grad_padded[slot_owner].reshape(fsdp_count, expert_local, capacity, model_width)
    grad_arrived = to_experts(grad_sent)
    grad_hidden = jnp.einsum(
        "secd,efd->secf", grad_arrived, down_full, preferred_element_type=jnp.float32
    )
    full_down_grad = jnp.einsum(
        "secf,secd->efd", hidden, grad_arrived, preferred_element_type=jnp.float32
    )
    grad_gate_val, grad_up_val = jax.vjp(swiglu, gate_val, up_val)[1](grad_hidden)
    grad_gate_low = grad_gate_val.astype(jnp.bfloat16)
    grad_up_low = grad_up_val.astype(jnp.bfloat16)
    full_gate_grad = jnp.einsum(
        "secd,secf->edf", arrived, grad_gate_low, preferred_element_type=jnp.float32
    )
    full_up_grad = jnp.einsum(
        "secd,secf->edf", arrived, grad_up_low, preferred_element_type=jnp.float32
    )
    grad_w_gate, grad_w_up, grad_w_down = (
        lax.psum_scatter(
            full_gate_grad.astype(jnp.bfloat16), "tp", scatter_dimension=2, tiled=True
        ).astype(jnp.float32),
        lax.psum_scatter(
            full_up_grad.astype(jnp.bfloat16), "tp", scatter_dimension=2, tiled=True
        ).astype(jnp.float32),
        lax.psum_scatter(
            full_down_grad.astype(jnp.bfloat16), "tp", scatter_dimension=1, tiled=True
        ).astype(jnp.float32),
    )
    grad_back = (
        jnp.einsum("secf,edf->secd", grad_gate_low, gate_full, preferred_element_type=jnp.float32)
        + jnp.einsum("secf,edf->secd", grad_up_low, up_full, preferred_element_type=jnp.float32)
    ).astype(jnp.bfloat16)
    grad_returned = from_experts(grad_back).reshape(experts * capacity, model_width)
    grad_from_slots = jnp.sum(
        grad_returned[slot_place].reshape(rows_local, top_count, model_width).astype(jnp.float32),
        axis=1,
    )
    grad_logits = jax.vjp(functools.partial(gate_pick, one_hot=one_hot_routes), logits)[1](
        grad_gates
    )[0].astype(jnp.bfloat16)
    grad_router_local = jnp.einsum(
        "td,te->de", ffn_normed, grad_logits, preferred_element_type=jnp.float32
    )
    grad_ffn_normed = grad_from_slots + jnp.einsum(
        "te,de->td", grad_logits, router_full, preferred_element_type=jnp.float32
    )
    grad_residual_part, grad_ffn_gain_local = jax.vjp(rms_norm, residual, ffn_gain_f)[1](
        grad_ffn_normed
    )
    grad_residual = cotangent + grad_residual_part
    grad_attn = (row_keep * grad_residual).astype(jnp.bfloat16)
    grad_attn_all = whole_group(grad_attn)
    grad_mixed = jnp.einsum(
        "gd,hd->gh", grad_attn_all, output_full, preferred_element_type=jnp.float32
    ).astype(jnp.bfloat16)
    grad_output_local = jnp.einsum(
        "gh,gd->hd", mixed_out, grad_attn_all, preferred_element_type=jnp.float32
    )
    grad_mixed_blocks = grad_mixed.reshape(block_count, block_rows, heads_local, HD)

    def backward_block(totals, block_in):
        key_total, value_total = totals
        query_block, grad_block, log_block = block_in
        scores = (
            jnp.einsum("qhd,khd->hqk", query_block, key_heads, preferred_element_type=jnp.float32)
            * score_scale
        )
        scores = jnp.where(key_valid[None, None, :], scores, -1e30)
        attn_prob = jnp.exp(scores - log_block[..., None])
        prob_low = attn_prob.astype(jnp.bfloat16)
        value_total = value_total + jnp.einsum(
            "hqk,qhd->khd", prob_low, grad_block, preferred_element_type=jnp.float32
        )
        grad_prob = jnp.einsum(
            "qhd,khd->hqk", grad_block, value_heads, preferred_element_type=jnp.float32
        )
        row_delta = jnp.sum(attn_prob * grad_prob, axis=-1, keepdims=True)
        grad_scores = (attn_prob * (grad_prob - row_delta)).astype(jnp.bfloat16)
        grad_query_block = (
            jnp.einsum("hqk,khd->qhd", grad_scores, key_heads, preferred_element_type=jnp.float32)
            * score_scale
        )
        key_total = (
            key_total
            + jnp.einsum(
                "hqk,qhd->khd", grad_scores, query_block, preferred_element_type=jnp.float32
            )
            * score_scale
        )
        return ((key_total, value_total), grad_query_block)

    zero_heads = jnp.zeros((group_rows, heads_local, HD), jnp.float32)
    (grad_key, grad_value), grad_query_blocks = lax.scan(
        backward_block, (zero_heads, zero_heads), (query_blocks, grad_mixed_blocks, log_totals)
    )
    grad_query = grad_query_blocks.reshape(group_rows, heads_local * HD)
    prepare_fn = functools.partial(head_prepare, cos_table=cos_table, sin_table=sin_table)
    grad_query_pre, grad_query_gain_local = jax.vjp(prepare_fn, query_pre, query_gain_f)[1](
        grad_query
    )
    grad_key_pre, grad_key_gain_local = jax.vjp(prepare_fn, key_pre, key_gain_f)[1](
        grad_key.reshape(group_rows, heads_local * HD)
    )
    grad_query_low = grad_query_pre.astype(jnp.bfloat16)
    grad_key_low = grad_key_pre.astype(jnp.bfloat16)
    grad_value_low = grad_value.reshape(group_rows, heads_local * HD).astype(jnp.bfloat16)
    grad_query_w = jnp.einsum(
        "gd,gh->dh", group_normed, grad_query_low, preferred_element_type=jnp.float32
    )
    grad_key_w = jnp.einsum(
        "gd,gh->dh", group_normed, grad_key_low, preferred_element_type=jnp.float32
    )
    grad_value_w = jnp.einsum(
        "gd,gh->dh", group_normed, grad_value_low, preferred_element_type=jnp.float32
    )

    def input_term(row_start, row_count):
        summed = jnp.einsum(
            "gh,dh->gd", grad_query_low, query_full, preferred_element_type=jnp.float32
        )
        summed = summed + jnp.einsum(
            "gh,dh->gd", grad_key_low, key_full, preferred_element_type=jnp.float32
        )
        return summed + jnp.einsum(
            "gh,dh->gd", grad_value_low, value_full, preferred_element_type=jnp.float32
        )

    grad_normed = head_sum(input_term, rows_local)
    grad_input_part, grad_attn_gain_local = jax.vjp(rms_norm, residual_in, attn_gain_f)[1](
        grad_normed
    )
    grad_input = grad_residual + grad_input_part
    grad_w_query, grad_w_key, grad_w_value, grad_w_output = (
        lax.psum_scatter(
            grad_query_w.astype(jnp.bfloat16), "fsdp", scatter_dimension=0, tiled=True
        ).astype(jnp.float32),
        lax.psum_scatter(
            grad_key_w.astype(jnp.bfloat16), "fsdp", scatter_dimension=0, tiled=True
        ).astype(jnp.float32),
        lax.psum_scatter(
            grad_value_w.astype(jnp.bfloat16), "fsdp", scatter_dimension=0, tiled=True
        ).astype(jnp.float32),
        lax.psum_scatter(
            grad_output_local.astype(jnp.bfloat16), "fsdp", scatter_dimension=1, tiled=True
        ).astype(jnp.float32),
    )
    grad_attn_gain, grad_query_gain, grad_key_gain, grad_ffn_gain, grad_router = (
        lax.psum_scatter(grad_attn_gain_local, ("fsdp", "tp"), scatter_dimension=0, tiled=True),
        lax.psum_scatter(grad_query_gain_local, ("fsdp", "tp"), scatter_dimension=0, tiled=True),
        lax.psum_scatter(grad_key_gain_local, ("fsdp", "tp"), scatter_dimension=0, tiled=True),
        lax.psum_scatter(grad_ffn_gain_local, ("fsdp", "tp"), scatter_dimension=0, tiled=True),
        lax.psum_scatter(grad_router_local, ("fsdp", "tp"), scatter_dimension=0, tiled=True),
    )
    return (
        block_out,
        grad_input,
        grad_attn_gain,
        grad_w_query,
        grad_w_key,
        grad_w_value,
        grad_query_gain,
        grad_key_gain,
        grad_w_output,
        grad_ffn_gain,
        grad_router,
        grad_w_gate,
        grad_w_up,
        grad_w_down,
    )


def solution(mesh):
    return jax.shard_map(
        per_device,
        mesh=mesh,
        in_specs=(
            P(("fsdp", "tp"), None),
            P("fsdp"),
            P("fsdp"),
            P(("fsdp", "tp"), None),
            P("fsdp"),
            P("fsdp", "tp"),
            P("fsdp", "tp"),
            P("fsdp", "tp"),
            P("fsdp"),
            P("fsdp"),
            P("tp", "fsdp"),
            P("fsdp"),
            P("fsdp", None),
            P("fsdp", None, "tp"),
            P("fsdp", None, "tp"),
            P("fsdp", "tp", None),
            P(("fsdp", "tp"), None),
        ),
        out_specs=(
            P(("fsdp", "tp"), None),
            P(("fsdp", "tp"), None),
            P(("fsdp", "tp")),
            P("fsdp", "tp"),
            P("fsdp", "tp"),
            P("fsdp", "tp"),
            P(("fsdp", "tp")),
            P(("fsdp", "tp")),
            P("tp", "fsdp"),
            P(("fsdp", "tp")),
            P(("fsdp", "tp"), None),
            P("fsdp", None, "tp"),
            P("fsdp", None, "tp"),
            P("fsdp", "tp", None),
        ),
        check_vma=False,
    )
```

profile of v0, /device:TPU:0, one launch (start us, length us, event | category | flops | bytes accessed | tf_op | source)
XLA Modules:
  0.0 2025.6 jit_solution(8894202204630522361)
XLA Ops:
  9.9 10.4 all-gather
  28.7 13.6 all-reduce.13
  47.6 76.4 %all-gather.12.cloned.1.call-done = bf16[1024,2048]{1,0:T(8,128)(2,1)} async-done(((bf16[256,2048]{1,0:T(8,128)(2,1)}), bf16[1024,2048]{1,0:T(8,128)(2,1)}) %all-gather.12.cloned.1.call-update) | async-done | bytes 4194320 | tf_op jit(solution)/shard_map/all_gather | solution.py:50
  124.0 6.6 multiply_reduce_fusion.9
  132.6 20.2 all-gather.16.cloned.1.call-done
  152.8 6.6 multiply_reduce_fusion.8
  174.0 5.0 fusion.86
  183.7 6.2 convolution_convert_fusion.6
  192.2 15.7 while.28
  207.8 4.9 all-gather.20.cloned.1.call-done
  212.8 6.3 convolution_convert_fusion
  227.9 8.8 all-gather.1
  236.8 4.5 reduce-window.6
  242.4 8.1 scatter_custom_fusion
  250.5 8.6 all_gather.51
  259.2 36.9 %reduce-scatter.13.cloned.1.call-done = bf16[256,2048]{1,0:T(8,128)(2,1)} async-done(((bf16[1024,2048]{1,0:T(8,128)(2,1)}), bf16[256,2048]{1,0:T(8,128)(2,1)}) %reduce-scatter.13.cloned.1.call-update) | async-done | bytes 1048592 | tf_op jit(solution)/shard_map/reduce_scatter | solution.py:54
  303.2 4.3 fusion.40
  307.5 9.1 concatenate.27
  316.6 22.8 %gather_fusion.2 = bf16[2304,2048]{1,0:T(8,128)(2,1)} fusion(bf16[2049,2048]{1,0:T(8,128)(2,1)} %concatenate.27, s32[3072]{0:T(1024)S(1)} %get-tuple-element.385), kind=kCustom, calls=%fused_computation.2 | custom fusion | bytes 18883584 | tf_op jit(solution)/shard_map/gather | solution.py:221
  339.5 5.1 all-to-all-start.2
  349.7 9.9 gather_fusion
  359.6 90.2 %all-to-all-done.2 = bf16[8,2,144,2048]{3,2,1,0:T(8,128)(2,1)} async-done(((bf16[8,2,144,2048]{3,2,1,0:T(8,128)(2,1)}), bf16[8,2,144,2048]{3,2,1,0:T(8,128)(2,1)}, u32[]{:S(2)}, u32[]{:S(2)}) %all-to-all-start.2) | async-done | bytes 9437216 | tf_op jit(solution)/shard_map/all_to_all | solution.py:63
  449.9 5.2 all-to-all-start
  455.1 18.5 fusion.58
  473.6 124.2 %all-gather.24.cloned.1.call-done = bf16[2,2048,1024]{2,1,0:T(8,128)(2,1)} async-done(((bf16[2,2048,256]{2,1,0:T(8,128)(2,1)}), bf16[2,2048,1024]{2,1,0:T(8,128)(2,1)}) %all-gather.24.cloned.1.call-update) | async-done | bytes 8388624 | tf_op jit(solution)/shard_map/all_gather | solution.py:200
  597.8 17.1 fusion.52
  614.8 132.4 %all-gather.22.cloned.1.call-done = bf16[2,2048,1024]{2,1,0:T(8,128)(2,1)} async-done(((bf16[2,2048,256]{2,1,0:T(8,128)(2,1)}), bf16[2,2048,1024]{2,1,0:T(8,128)(2,1)}) %all-gather.22.cloned.1.call-update) | async-done | bytes 8388624 | tf_op jit(solution)/shard_map/all_gather | solution.py:199
  747.2 24.6 %fusion.43 = (bf16[8,2,144,1024]{3,2,0,1:T(8,128)(2,1)}, bf16[8,2,144,1024]{3,2,0,1:T(8,128)(2,1)}, bf16[8,2,144,1024]{3,2,0,1:T(8,128)(2,1)}) fusion(f32[2,8,144,1024]{3,2,1,0:T(8,128)} %fusion.52, f32[2,8,144,1024]{3,2,1,0:T(8,128)} %fusion.58, bf16[2,2048,1024]{2,1,0:T(8,128)(2,1)} %all-gather.22.cloned.1.call-done, ...), kind=kOutput, calls=%fused_computation.70 | convolution fusion | flops 9701425152 | bytes 50855936 | tf_op jit(solution)/shard_map/secd,edf->secf/dot_general | solution.py:203
  771.8 16.4 convert_bitcast_fusion
  788.2 9.2 copy.207
  797.4 5.4 all-to-all-start.1
  802.8 17.4 fusion.50
  820.3 18.6 fusion.44
  838.9 9.3 copy.210
  848.2 59.9 %all-to-all-done.1 = bf16[8,2,144,2048]{3,2,1,0:T(8,128)(2,1)} async-done(((bf16[8,2,144,2048]{3,2,1,0:T(8,128)(2,1)}), bf16[8,2,144,2048]{3,2,1,0:T(8,128)(2,1)}, u32[]{:S(2)}, u32[]{:S(2)}) %all-to-all-start.1) | async-done | bytes 9437216 | tf_op jit(solution)/shard_map/all_to_all | solution.py:67
  908.1 5.0 all-to-all-start.3
  913.3 21.5 %gather_fusion.1 = bf16[2048,2048]{1,0:T(8,128)(2,1)} fusion(bf16[2304,2048]{1,0:T(8,128)(2,1)} %bitcast.29, s32[2048]{0:T(1024)S(1)} %broadcast_clamp_fusion), kind=kCustom, calls=%fused_computation.1 | custom fusion | bytes 16785408 | tf_op jit(solution)/shard_map/gather | solution.py:210
  934.8 9.5 fusion.39
  944.5 74.0 %all-to-all-done.3 = bf16[8,2,144,2048]{3,2,1,0:T(8,128)(2,1)} async-done(((bf16[8,2,144,2048]{3,2,1,0:T(8,128)(2,1)}), bf16[8,2,144,2048]{3,2,1,0:T(8,128)(2,1)}, u32[]{:S(2)}, u32[]{:S(2)}) %all-to-all-start.3) | async-done | bytes 9437216 | tf_op jit(solution)/shard_map/all_to_all | solution.py:67
  1018.4 21.3 %gather_fusion.3 = bf16[2048,2048]{1,0:T(8,128)(2,1)} fusion(bf16[2304,2048]{1,0:T(8,128)(2,1)} %bitcast.38, s32[2048]{0:T(1024)S(1)} %broadcast_clamp_fusion), kind=kCustom, calls=%fused_computation.3 | custom fusion | bytes 16785408 | tf_op jit(solution)/shard_map/gather | solution.py:255
  1039.8 11.4 convert_reduce_fusion
  1059.5 18.7 bitcast_convert_fusion
  1078.2 17.1 bitcast_convert_fusion.2
  1095.4 17.6 bitcast_convert_fusion.1
  1113.1 23.6 %all-gather.28.cloned.1.call-done = bf16[1024,2048]{1,0:T(8,128)(2,1)} async-done(((bf16[256,2048]{1,0:T(8,128)(2,1)}), bf16[1024,2048]{1,0:T(8,128)(2,1)}) %all-gather.28.cloned.1.call-update) | async-done | bytes 4194320 | tf_op jit(solution)/shard_map/all_gather | solution.py:50
  1136.6 6.2 convolution_convert_fusion.5
  1145.2 40.2 %while.29 = (s32[]{:T(128)}, f32[1024,4,128]{0,2,1:T(8,128)S(1)}, f32[1024,4,128]{0,2,1:T(8,128)}, f32[2,512,4,128]{3,1,0,2:T(8,128)}, bf16[2,512,4,128]{3,1,2,0...) while((s32[]{:T(128)}, f32[1024,4,128]{0,2,1:T(8,128)S(1)}, ...), condition=%wide.region_24.25_spmd.clone, body=%wide.region_22.24_spmd.clone.sunk | while | flops 2718696448 | bytes 175175536 | solution.py:313
  1181.0 4.5 bitcast_add_fusion.5
  1194.0 4.7 multiply_reduce_fusion.2
  1201.7 6.3 convolution_convert_fusion.3
  1208.0 6.3 convolution_convert_fusion.1
  1218.8 6.3 convolution_convert_fusion.4
  1226.9 5.9 convolution_convert_fusion.2
  1240.6 6.1 add_convert_fusion.1
  1246.7 27.8 %reduce-scatter.31.cloned.1.call-done = f32[64,16]{1,0:T(8,128)} async-done(((f32[2048,16]{1,0:T(8,128)}), f32[64,16]{1,0:T(8,128)}) %reduce-scatter.31.cloned.1.call-update) | async-done | bytes 4112
  1275.9 142.1 %reduce-scatter.29.cloned.1.call-done = bf16[2,256,2048]{2,1,0:T(8,128)(2,1)} async-done(((bf16[2,1024,2048]{2,1,0:T(8,128)(2,1)}), bf16[2,256,2048]{2,1,0:T(8,128)(2,1)}) %reduce-scatter.29.cloned.1.call-update) | async-done | bytes 2097168 | tf_op jit(solution)/shard_map/reduce_scatter | solution.py:245
  1422.1 143.5 %reduce-scatter.25.cloned.1.call-done = bf16[2,2048,256]{2,1,0:T(8,128)(2,1)} async-done(((bf16[2,2048,1024]{2,1,0:T(8,128)(2,1)}), bf16[2,2048,256]{2,1,0:T(8,128)(2,1)}) %reduce-scatter.25.cloned.1.call-update) | async-done | bytes 2097168 | tf_op jit(solution)/shard_map/reduce_scatter | solution.py:239
  1569.5 143.5 %reduce-scatter.27.cloned.1.call-done = bf16[2,2048,256]{2,1,0:T(8,128)(2,1)} async-done(((bf16[2,2048,1024]{2,1,0:T(8,128)(2,1)}), bf16[2,2048,256]{2,1,0:T(8,128)(2,1)}) %reduce-scatter.27.cloned.1.call-update) | async-done | bytes 2097168 | tf_op jit(solution)/shard_map/reduce_scatter | solution.py:242
  1717.0 41.0 %reduce-scatter.19.cloned.1.call-done = bf16[256,512]{1,0:T(8,128)(2,1)} async-done(((bf16[2048,512]{1,0:T(8,128)(2,1)}), bf16[256,512]{1,0:T(8,128)(2,1)}) %reduce-scatter.19.cloned.1.call-update) | async-done | bytes 262160 | tf_op jit(solution)/shard_map/reduce_scatter | solution.py:357
  1759.8 42.5 %reduce-scatter.23.cloned.1.call-done = bf16[512,256]{1,0:T(8,128)(2,1)} async-done(((bf16[512,2048]{1,0:T(8,128)(2,1)}), bf16[512,256]{1,0:T(8,128)(2,1)}) %reduce-scatter.23.cloned.1.call-update) | async-done | bytes 262160 | tf_op jit(solution)/shard_map/reduce_scatter | solution.py:363
  1804.0 42.5 %reduce-scatter.17.cloned.1.call-done = bf16[256,512]{1,0:T(8,128)(2,1)} async-done(((bf16[2048,512]{1,0:T(8,128)(2,1)}), bf16[256,512]{1,0:T(8,128)(2,1)}) %reduce-scatter.17.cloned.1.call-update) | async-done | bytes 262160 | tf_op jit(solution)/shard_map/reduce_scatter | solution.py:354
  1848.3 42.5 %reduce-scatter.21.cloned.1.call-done = bf16[256,512]{1,0:T(8,128)(2,1)} async-done(((bf16[2048,512]{1,0:T(8,128)(2,1)}), bf16[256,512]{1,0:T(8,128)(2,1)}) %reduce-scatter.21.cloned.1.call-update) | async-done | bytes 262160 | tf_op jit(solution)/shard_map/reduce_scatter | solution.py:360
  1892.6 77.3 %reduce-scatter.15.cloned.1.call-done = bf16[256,2048]{1,0:T(8,128)(2,1)} async-done(((bf16[1024,2048]{1,0:T(8,128)(2,1)}), bf16[256,2048]{1,0:T(8,128)(2,1)}) %reduce-scatter.15.cloned.1.call-update) | async-done | bytes 1048592 | tf_op jit(solution)/shard_map/reduce_scatter | solution.py:54
  1972.2 41.0 %all-reduce.12 = (f32[2048]{0:T(1024)S(1)}, f32[128]{0:T(128)S(1)}, f32[128]{0:T(128)S(1)}, f32[2048]{0:T(1024)S(1)}) all-reduce(f32[2048]{0:T(1024)S(1)} %get-tuple-element.293, f32[128]{0:T(128)S(1)} %get-tuple-element.360, f32[128]{0:T(128)S(1)} %get-tuple-element.289, ...), channel_id=4, replica_groups=mesh['fsdp'=8,'tp'=4] {'fsdp','tp'}, use_global_device_ids=true, to_apply=%region_30.31.clone | all-reduce | flops 4352 | bytes 34816
  (384 shorter events, 175.6 us)
Async XLA Ops:
  7.2 15.9 copy-start.6
  7.2 40.4 %all-gather.14.cloned.1.call-start = ((), (), s32[]{:S(2)}) async-start(), calls=%async_computation.15 | async-start | bytes 2359296 | tf_op jit(solution)/shard_map/all_gather | solution.py:126
  9.1 114.9 %all-gather.12.cloned.1.call-start = ((), (), s32[]{:S(2)}) async-start(), calls=%async_computation.14 | async-start | bytes 5242880 | tf_op jit(solution)/shard_map/all_gather | solution.py:50
  24.4 128.4 %all-gather.16.cloned.1.call-start = ((), (), s32[]{:S(2)}) async-start(), calls=%async_computation.16 | async-start | bytes 2359296 | tf_op jit(solution)/shard_map/all_gather | solution.py:127
  25.2 158.5 %all-gather.18.cloned.1.call-start = ((), (), s32[]{:S(2)}) async-start(), calls=%async_computation.17 | async-start | bytes 2359296 | tf_op jit(solution)/shard_map/all_gather | solution.py:128
  26.0 186.8 %all-gather.20.cloned.1.call-start = ((), (), s32[]{:S(2)}) async-start(), calls=%async_computation.18 | async-start | bytes 2359296 | tf_op jit(solution)/shard_map/all_gather | solution.py:129
  26.8 269.2 %reduce-scatter.13.cloned.1.call-start = ((), (), s32[]{:S(2)}) async-start(), calls=%async_computation.19 | async-start | bytes 5242880 | tf_op jit(solution)/shard_map/reduce_scatter | solution.py:54
  42.3 120.6 %copy-start.81 = (f32[128]{0:T(128)}, f32[128]{0:T(128)S(1)}, u32[]{:S(2)}) copy-start(f32[128]{0:T(128)S(1)} %convert_element_type.233) | copy-start | bytes 1540
  42.3 121.4 %copy-start.83 = (f32[128]{0:T(128)}, f32[128]{0:T(128)S(1)}, u32[]{:S(2)}) copy-start(f32[128]{0:T(128)S(1)} %convert_element_type.238) | copy-start | bytes 1540
  45.9 84.7 %copy-start.33 = (f32[1024,128]{1,0:T(8,128)}, f32[1024,128]{1,0:T(8,128)S(1)}, u32[]{:S(2)}) copy-start(f32[1024,128]{1,0:T(8,128)S(1)} %get-tuple-element.368) | copy-start | bytes 1572868
  130.6 43.4 %copy-start.47 = (f32[1024,4]{0,1:T(4,128)}, f32[1024,4]{0,1:T(4,128)S(1)}, u32[]{:S(2)}) copy-start(f32[1024,4]{0,1:T(4,128)S(1)} %fusion.102) | copy-start | bytes 49156
  132.6 30.3 %copy-start.13 = (f32[1024,4,128]{2,0,1:T(8,128)}, f32[1024,4,128]{2,0,1:T(8,128)S(1)}, u32[]{:S(2)}) copy-start(f32[1024,4,128]{2,0,1:T(8,128)S(1)} %copy.192) | copy-start | bytes 6291460
  160.0 14.1 copy-start.49
  207.8 11.2 copy-start.3
  207.8 11.2 copy-start.5
  207.8 11.2 copy-start.57
  219.1 236.0 %all-gather.26.cloned.1.call-start = ((), (), s32[]{:S(2)}) async-start(), calls=%async_computation.22 | async-start | bytes 10485760 | tf_op jit(solution)/shard_map/all_gather | solution.py:201
  223.0 374.8 %all-gather.24.cloned.1.call-start = ((), (), s32[]{:S(2)}) async-start(), calls=%async_computation.21 | async-start | bytes 10485760 | tf_op jit(solution)/shard_map/all_gather | solution.py:200
  226.8 9.9 copy-start.76
  236.7 64.1 %copy-start.53 = (f32[8,1,256]{2,1,0:T(1,128)}, f32[8,1,256]{2,1,0:T(1,128)S(1)}, u32[]{:S(2)}) copy-start(f32[8,1,256]{2,1,0:T(1,128)S(1)} %convert_element_type.294) | copy-start | bytes 24580
  242.4 16.7 copy-start.64
  259.1 41.8 %copy-start.40 = (bf16[2048,16]{0,1:T(8,128)(2,1)}, bf16[2048,16]{0,1:T(8,128)(2,1)S(1)}, u32[]{:S(2)}) copy-start(bf16[2048,16]{0,1:T(8,128)(2,1)S(1)} %all_gather.51) | copy-start | bytes 196612
  259.1 41.7 %copy-start.66 = (f32[256]{0:T(256)}, f32[256]{0:T(256)S(1)}, u32[]{:S(2)}) copy-start(f32[256]{0:T(256)S(1)} %and_convert_fusion) | copy-start | bytes 3076
  300.9 6.6 copy-start.17
  302.3 5.2 copy-start.68
  302.3 5.2 copy-start.74
  339.5 110.4 %all-to-all-start.2 = ((bf16[8,2,144,2048]{3,2,1,0:T(8,128)(2,1)}), bf16[8,2,144,2048]{3,2,1,0:T(8,128)(2,1)}, u32[]{:S(2)}, u32[]{:S(2)}) async-start(bf16[8,2,144,2048]{3,2,1,0:T(8,128)(2,1)} %bitcast.283), calls=%async_computation.3 | async-start | bytes 18874368 | tf_op jit(solution)/shard_map/all_to_all | solution.py:63
  344.6 402.7 %all-gather.22.cloned.1.call-start = ((), (), s32[]{:S(2)}) async-start(), calls=%async_computation.20 | async-start | bytes 10485760 | tf_op jit(solution)/shard_map/all_gather | solution.py:199
  449.9 147.9 %all-to-all-start = ((bf16[8,2,144,2048]{3,2,1,0:T(8,128)(2,1)}), bf16[8,2,144,2048]{3,2,1,0:T(8,128)(2,1)}, u32[]{:S(2)}, u32[]{:S(2)}) async-start(bf16[8,2,144,2048]{3,2,1,0:T(8,128)(2,1)} %bitcast.284), calls=%async_computation.1 | async-start | bytes 18874368 | tf_op jit(solution)/shard_map/all_to_all | solution.py:63
  797.4 110.7 %all-to-all-start.1 = ((bf16[8,2,144,2048]{3,2,1,0:T(8,128)(2,1)}), bf16[8,2,144,2048]{3,2,1,0:T(8,128)(2,1)}, u32[]{:S(2)}, u32[]{:S(2)}) async-start(bf16[8,2,144,2048]{3,2,1,0:T(8,128)(2,1)} %copy.207), calls=%async_computation.2 | async-start | bytes 18874368 | tf_op jit(solution)/shard_map/all_to_all | solution.py:67
  848.2 65.0 %copy-start.65 = (s32[2048,1]{0,1:T(1,128)S(1)}, s32[2048,1]{0,1:T(1,128)}, u32[]{:S(2)}) copy-start(s32[2048,1]{0,1:T(1,128)} %copy-done.64) | copy-start | bytes 24580
  848.2 65.0 %copy-start.75 = (f32[256]{0:T(256)S(1)}, f32[256]{0:T(256)}, u32[]{:S(2)}) copy-start(f32[256]{0:T(256)} %copy-done.74) | copy-start | bytes 3076
  908.1 110.3 %all-to-all-start.3 = ((bf16[8,2,144,2048]{3,2,1,0:T(8,128)(2,1)}), bf16[8,2,144,2048]{3,2,1,0:T(8,128)(2,1)}, u32[]{:S(2)}, u32[]{:S(2)}) async-start(bf16[8,2,144,2048]{3,2,1,0:T(8,128)(2,1)} %copy.210), calls=%async_computation.4 | async-start | bytes 18874368 | tf_op jit(solution)/shard_map/all_to_all | solution.py:67
  913.2 223.5 %all-gather.28.cloned.1.call-start = ((), (), s32[]{:S(2)}) async-start(), calls=%async_computation.23 | async-start | bytes 5242880 | tf_op jit(solution)/shard_map/all_gather | solution.py:50
  913.3 21.5 %copy-start.18 = (f32[256,2048]{1,0:T(8,128)S(1)}, f32[256,2048]{1,0:T(8,128)}, u32[]{:S(2)}) copy-start(f32[256,2048]{1,0:T(8,128)} %copy-done.17) | copy-start | bytes 6291460
  913.3 21.5 %copy-start.36 = (f32[256,8]{1,0:T(8,128)S(1)}, f32[256,8]{1,0:T(8,128)}, u32[]{:S(2)}) copy-start(f32[256,8]{1,0:T(8,128)} %copy-done.35) | copy-start | bytes 24580
  934.8 9.6 copy-start.56
  934.8 9.6 copy-start.46
  934.8 9.6 copy-start.69
  1039.7 11.5 copy-start.7
  1039.7 11.5 copy-start.21
  1039.7 11.5 copy-start.41
  1039.7 11.5 copy-start.54
  1039.8 11.5 copy-start.67
  1039.8 11.5 copy-start.73
  1057.8 216.7 %reduce-scatter.31.cloned.1.call-start = ((), (), s32[]{:S(2)}) async-start(), calls=%async_computation.32 | async-start | bytes 1081344
  1059.4 358.5 %reduce-scatter.29.cloned.1.call-start = ((), (), s32[]{:S(2)}) async-start(), calls=%async_computation.31 | async-start | bytes 10485760 | tf_op jit(solution)/shard_map/reduce_scatter | solution.py:245
  1078.2 487.4 %reduce-scatter.25.cloned.1.call-start = ((), (), s32[]{:S(2)}) async-start(), calls=%async_computation.29 | async-start | bytes 10485760 | tf_op jit(solution)/shard_map/reduce_scatter | solution.py:239
  1095.4 617.7 %reduce-scatter.27.cloned.1.call-start = ((), (), s32[]{:S(2)}) async-start(), calls=%async_computation.30 | async-start | bytes 10485760 | tf_op jit(solution)/shard_map/reduce_scatter | solution.py:242
  1113.0 645.0 %reduce-scatter.19.cloned.1.call-start = ((), (), s32[]{:S(2)}) async-start(), calls=%async_computation.26 | async-start | bytes 2359296 | tf_op jit(solution)/shard_map/reduce_scatter | solution.py:357
  1154.7 6.2 copy-start.1
  1174.2 6.2 copy-start.1
  1194.0 4.7 copy-start.62
  1208.0 594.3 %reduce-scatter.23.cloned.1.call-start = ((), (), s32[]{:S(2)}) async-start(), calls=%async_computation.28 | async-start | bytes 2359296 | tf_op jit(solution)/shard_map/reduce_scatter | solution.py:363
  1214.4 632.2 %reduce-scatter.17.cloned.1.call-start = ((), (), s32[]{:S(2)}) async-start(), calls=%async_computation.25 | async-start | bytes 2359296 | tf_op jit(solution)/shard_map/reduce_scatter | solution.py:354
  1218.8 6.3 copy-start.38
  1225.1 665.7 %reduce-scatter.21.cloned.1.call-start = ((), (), s32[]{:S(2)}) async-start(), calls=%async_computation.27 | async-start | bytes 2359296 | tf_op jit(solution)/shard_map/reduce_scatter | solution.py:360
  1232.8 737.1 %reduce-scatter.15.cloned.1.call-start = ((), (), s32[]{:S(2)}) async-start(), calls=%async_computation.24 | async-start | bytes 5242880 | tf_op jit(solution)/shard_map/reduce_scatter | solution.py:54
  1717.0 252.9 %copy-start.8 = (bf16[256,2048]{1,0:T(8,128)(2,1)S(1)}, bf16[256,2048]{1,0:T(8,128)(2,1)}, u32[]{:S(2)}) copy-start(bf16[256,2048]{1,0:T(8,128)(2,1)} %param.21) | copy-start | bytes 3145732
  1717.0 252.9 %copy-start.52 = (f32[8,1,256]{2,1,0:T(1,128)S(1)}, f32[8,1,256]{2,1,0:T(1,128)}, u32[]{:S(2)}) copy-start(f32[8,1,256]{2,1,0:T(1,128)} %copy-done.51) | copy-start | bytes 24580
  1717.0 252.9 %copy-start.71 = (f32[256]{0:T(256)S(1)}, f32[256]{0:T(256)}, u32[]{:S(2)}) copy-start(f32[256]{0:T(256)} %copy-done.70) | copy-start | bytes 3076
  1759.8 212.4 %copy-start.63 = (f32[2048]{0:T(1024)S(1)}, f32[2048]{0:T(1024)}, u32[]{:S(2)}) copy-start(f32[2048]{0:T(1024)} %get-tuple-element.287) | copy-start | bytes 24580
  1759.8 255.7 %copy-start.80 = (f32[256]{0:T(256)S(1)}, f32[256]{0:T(256)}, u32[]{:S(2)}) copy-start(f32[256]{0:T(256)} %copy-done.79) | copy-start | bytes 3076
  1759.8 255.7 %copy-start.27 = (f32[256,2048]{1,0:T(8,128)S(1)}, f32[256,2048]{1,0:T(8,128)}, u32[]{:S(2)}) copy-start(f32[256,2048]{1,0:T(8,128)} %get-tuple-element.342) | copy-start | bytes 6291460
  (57 other events, 137.1 us)
Sparse Core Ops, SparseCore 0:
  10.5 30.6 all-gather.13
  43.3 80.6 all-gather.11
  126.5 26.2 all-gather.15
  154.5 27.7 all-gather.17
  184.6 28.0 all-gather.19
  219.2 76.7 reduce-scatter.12
  298.2 150.0 all-gather.25
  450.5 147.2 all-gather.23
  599.9 147.2 all-gather.21
  1057.9 78.6 all-gather.27
  1138.9 135.5 reduce-scatter.30
  1276.7 141.2 reduce-scatter.28
  1420.3 145.2 reduce-scatter.24
  1567.8 145.2 reduce-scatter.26
  1716.2 41.7 reduce-scatter.18
  1761.1 41.0 reduce-scatter.22
  1805.4 41.1 reduce-scatter.16
  1849.7 41.1 reduce-scatter.20
  1893.1 76.7 reduce-scatter.14
where the time goes:
time: 2040 us; the launch traced here: 2030 us
  waiting for transfers between devices  1350 us (66%)
  matrix products  278 us (14%)
  local copies, waits for them, and re-layouts  157 us (8%)
  other arithmetic  123 us (6%)
  blocking collectives  82.4 us (4%)
  starting transfers between devices  21.9 us (1%)
    reduce_scatter x1, waiting for transfers between devices, per_device(): lax.psum_scatter(full_up_grad.astype(jnp.bfloat16), 'tp', scatter_dimensi...  144 us
    reduce_scatter x1, waiting for transfers between devices, per_device(): lax.psum_scatter(full_gate_grad.astype(jnp.bfloat16), 'tp', scatter_dimen...  143 us
    reduce_scatter x1, waiting for transfers between devices, per_device(): lax.psum_scatter(full_down_grad.astype(jnp.bfloat16), 'tp', scatter_dimen...  142 us
    all_to_all x2, waiting for transfers between devices, from_experts(): lax.all_to_all(buffer, 'fsdp', split_axis=0, concat_axis=0, tiled=True)  134 us
    all_gather x1, waiting for transfers between devices, per_device(): lax.all_gather(gate_local, 'tp', axis=2, tiled=True)  132 us
    all_gather x1, waiting for transfers between devices, per_device(): lax.all_gather(up_local, 'tp', axis=2, tiled=True)  124 us
    reduce_scatter x2, waiting for transfers between devices, head_sum(): lax.psum_scatter(term_fn(jnp.int32(0), lax.axis_size('tp') * rows_local)....  114 us
    all_gather x2, waiting for transfers between devices, whole_group(): return lax.all_gather(values, 'tp', axis=0, tiled=True)  100 us
  transfers between devices with their start and end apart: 23, of which 19 were waited for; matrix products, arithmetic and copies ran while one was open for 22% of the time, Pallas kernels for 0%

commit v1 on v0

--- a/solution.py
+++ b/solution.py
@@ -67,7 +67,7 @@
     return lax.all_to_all(buffer, "fsdp", split_axis=0, concat_axis=0, tiled=True)
 
 
-def per_device(
+def per_device_routed(
     hidden_in,
     seq_lengths,
     seq_offsets,
@@ -389,6 +389,423 @@
     )
 
 
+def pair_swap(values, distance):
+    count = lax.axis_size("tp")
+    return lax.ppermute(values, "tp", [(i, i ^ distance) for i in range(count)])
+
+
+def shift_tp(values, step, first, last):
+    return lax.ppermute(values, "tp", [(i, i + step) for i in range(first, last + 1)])
+
+
+def line_gather(values):
+    right, left, from_left, from_right = (values, values, [], [])
+    for step in range(3):
+        right = shift_tp(right, 1, step, 2)
+        left = shift_tp(left, -1, 1, 3 - step)
+        from_left.append(right)
+        from_right.append(left)
+    place = lax.axis_index("tp")
+    blocks = [values]
+    for offset in range(1, 4):
+        blocks.append(jnp.where(place >= offset, from_left[offset - 1], from_right[3 - offset]))
+    return jnp.concatenate(blocks, axis=0)
+
+
+def line_scatter(blocks):
+    right, left = (None, None)
+    for step in range(3):
+        to_right, to_left = (blocks[step + 1], blocks[3 - step])
+        if step > 0:
+            to_right = to_right.astype(jnp.float32) + right.astype(jnp.float32)
+            to_left = to_left.astype(jnp.float32) + left.astype(jnp.float32)
+        right = shift_tp(to_right.astype(jnp.bfloat16), 1, 0, step)
+        left = shift_tp(to_left.astype(jnp.bfloat16), -1, 3 - step, 3)
+    return (
+        blocks[0].astype(jnp.float32) + right.astype(jnp.float32) + left.astype(jnp.float32)
+    )
+
+
+def gather_plane(values):
+    return lax.all_gather(values, "fsdp", axis=0, tiled=True)
+
+
+def scatter_plane(values):
+    return lax.psum_scatter(values, "fsdp", scatter_dimension=0, tiled=True)
+
+
+def matmul(left, right, left_dim, right_dim):
+    return lax.dot_general(
+        left,
+        right,
+        (((left_dim,), (right_dim,)), ((), ())),
+        preferred_element_type=jnp.float32,
+    )
+
+
+def per_device_dense(
+    hidden_in,
+    seq_lengths,
+    seq_offsets,
+    routes,
+    attn_gain,
+    w_query,
+    w_key,
+    w_value,
+    query_gain,
+    key_gain,
+    w_output,
+    ffn_gain,
+    router,
+    w_gate,
+    w_up,
+    w_down,
+    cotangent,
+):
+    low = jnp.bfloat16
+    full = jnp.float32
+    tp_size = lax.axis_size("tp")
+    fsdp_size = lax.axis_size("fsdp")
+    tp_place = lax.axis_index("tp")
+    fsdp_place = lax.axis_index("fsdp")
+    rows, width = hidden_in.shape
+    group_rows = rows * tp_size
+    experts = router.shape[1]
+    expert_local = w_gate.shape[0]
+    quarter = w_gate.shape[2]
+    shard = w_query.shape[0]
+    head_width = w_query.shape[1]
+    heads = head_width // HD
+    block_rows = min(512, group_rows)
+    block_count = group_rows // block_rows
+    score_scale = HD ** (-0.5)
+    seq_start = seq_offsets[0]
+    seq_end = seq_start + seq_lengths[0]
+
+    group_hidden = line_gather(hidden_in)
+    order = jnp.mod(tp_place - jnp.arange(tp_size, dtype=jnp.int32), tp_size)
+    group_place = (
+        order[:, None] * rows + jnp.arange(rows, dtype=jnp.int32)[None, :]
+    ).reshape(group_rows)
+    key_valid = (group_place >= seq_start) & (group_place < seq_end)
+    row_keep = key_valid[:rows].astype(full)[:, None]
+    cos_table, sin_table = rotary_tables(group_place - seq_start, HD)
+
+    small = jnp.zeros((shard, 128), low)
+    small = small.at[:, :experts].set(router.astype(low))
+    small = small.at[:, experts].set(attn_gain.astype(low))
+    small = small.at[:, experts + 1].set(ffn_gain.astype(low))
+    small = small.at[: query_gain.shape[0], experts + 2].set(query_gain.astype(low))
+    small = small.at[: key_gain.shape[0], experts + 3].set(key_gain.astype(low))
+    packed = jnp.concatenate(
+        [
+            w_query.astype(low),
+            w_key.astype(low),
+            w_value.astype(low),
+            w_output.astype(low).T,
+            small,
+        ],
+        axis=1,
+    )
+    packed_full = gather_plane(packed)
+    w_qkv = packed_full[:, : 3 * head_width]
+    w_out_t = packed_full[:, 3 * head_width : 4 * head_width]
+    small_full = packed_full[:, 4 * head_width :]
+    small_t = small_full.T
+    router_full = small_full[:, :experts]
+    attn_gain_f = small_t[experts].astype(full)
+    ffn_gain_f = small_t[experts + 1].astype(full)
+    gain_piece = query_gain.shape[0]
+    query_gain_f = small_t[experts + 2].reshape(fsdp_size, shard)[:, :gain_piece].reshape(-1)
+    key_gain_f = small_t[experts + 3].reshape(fsdp_size, shard)[:, :gain_piece].reshape(-1)
+    query_gain_f = query_gain_f.astype(full)
+    key_gain_f = key_gain_f.astype(full)
+
+    expert_ids = jnp.arange(experts, dtype=jnp.int32)
+    own_mask = jnp.sum(
+        (routes[:, :, None] == expert_ids[None, None, :]).astype(full), axis=1
+    ) * row_keep
+    mask_low = own_mask.astype(low)
+    grad_low = cotangent.astype(low)
+    mask_parts = [gather_plane(mask_low), gather_plane(pair_swap(mask_low, 2))]
+    grad_parts = [gather_plane(grad_low), gather_plane(pair_swap(grad_low, 2))]
+
+    gate_own = jnp.concatenate([w_gate[e] for e in range(expert_local)], axis=1).astype(low)
+    up_own = jnp.concatenate([w_up[e] for e in range(expert_local)], axis=1).astype(low)
+    down_own = w_down.reshape(expert_local * quarter, width).astype(low)
+    gate_all = jnp.concatenate([gate_own, pair_swap(gate_own, 1)], axis=1)
+    up_all = jnp.concatenate([up_own, pair_swap(up_own, 1)], axis=1)
+    down_all = jnp.concatenate([down_own, pair_swap(down_own, 1)], axis=0)
+
+    group_full = group_hidden.astype(full)
+    row_scale = lax.rsqrt(jnp.mean(group_full * group_full, axis=-1, keepdims=True) + NORM_EPSILON)
+    group_normed = (group_full * row_scale * attn_gain_f).astype(low)
+    qkv_pre = matmul(group_normed, w_qkv, 1, 0)
+    query_pre = qkv_pre[:, :head_width]
+    key_pre = qkv_pre[:, head_width : 2 * head_width]
+    value_low = qkv_pre[:, 2 * head_width :].astype(low)
+    query_low = head_prepare(query_pre, query_gain_f, cos_table, sin_table).astype(low)
+    key_low = head_prepare(key_pre, key_gain_f, cos_table, sin_table).astype(low)
+    key_heads = key_low.reshape(group_rows, heads, HD)
+    value_heads = value_low.reshape(group_rows, heads, HD)
+    query_blocks = query_low.reshape(block_count, block_rows, heads, HD)
+
+    def forward_block(query_block):
+        scores = (
+            jnp.einsum("qhd,khd->hqk", query_block, key_heads, preferred_element_type=full)
+            * score_scale
+        )
+        scores = jnp.where(key_valid[None, None, :], scores, -1e30)
+        row_max = jnp.max(scores, axis=-1, keepdims=True)
+        exp_scores = jnp.exp(scores - row_max)
+        row_total = jnp.sum(exp_scores, axis=-1, keepdims=True)
+        attn_prob = (exp_scores / row_total).astype(low)
+        mixed_block = jnp.einsum(
+            "hqk,khd->qhd", attn_prob, value_heads, preferred_element_type=full
+        )
+        return (mixed_block.astype(low), (row_max + jnp.log(row_total))[..., 0])
+
+    mixed_blocks, log_totals = lax.map(forward_block, query_blocks)
+    mixed_out = mixed_blocks.reshape(group_rows, heads * HD)
+    attn_term = matmul(mixed_out, w_out_t, 1, 1).astype(low)
+    attn_out = line_scatter([attn_term[k * rows : (k + 1) * rows] for k in range(tp_size)])
+    hidden_full = hidden_in.astype(full)
+    residual = hidden_full + row_keep * attn_out
+    ffn_scale = lax.rsqrt(jnp.mean(residual * residual, axis=-1, keepdims=True) + NORM_EPSILON)
+    ffn_normed = (residual * ffn_scale * ffn_gain_f).astype(low)
+    row_parts = [gather_plane(ffn_normed), gather_plane(pair_swap(ffn_normed, 2))]
+    probs = jax.nn.softmax(matmul(ffn_normed, router_full, 1, 0), axis=-1)
+
+    saved = []
+    gate_grads = []
+    for part in range(2):
+        part_rows, part_grad, part_mask = (row_parts[part], grad_parts[part], mask_parts[part])
+        part_gate = jax.nn.softmax(matmul(part_rows, router_full, 1, 0), axis=-1) * part_mask
+        chosen = [
+            (expert_ids == fsdp_place * expert_local + e).astype(full)[None, :]
+            for e in range(expert_local)
+        ]
+        gates = [jnp.sum(part_gate * pick, axis=1, keepdims=True) for pick in chosen]
+        masks = [jnp.sum(part_mask.astype(full) * pick, axis=1) for pick in chosen]
+        spread = jnp.concatenate(
+            [
+                jnp.broadcast_to(gates[e], (gates[e].shape[0], quarter))
+                for _ in range(2)
+                for e in range(expert_local)
+            ],
+            axis=1,
+        )
+        gate_val = matmul(part_rows, gate_all, 1, 0)
+        up_val = matmul(part_rows, up_all, 1, 0)
+        grad_hidden = matmul(part_grad, down_all, 1, 1)
+        sigma = jax.nn.sigmoid(gate_val)
+        silu = gate_val * sigma
+        hidden = (silu * up_val).astype(low)
+        product = hidden.astype(full) * grad_hidden
+        gate_grads.append(
+            jnp.stack(
+                [
+                    jnp.sum(
+                        product[:, e * quarter : (e + 1) * quarter]
+                        + product[
+                            :, (expert_local + e) * quarter : (expert_local + e + 1) * quarter
+                        ],
+                        axis=1,
+                    )
+                    * masks[e]
+                    for e in range(expert_local)
+                ],
+                axis=0,
+            )
+        )
+        scaled = spread * grad_hidden
+        grad_gate_low = (scaled * up_val * (sigma * (1.0 + gate_val * (1.0 - sigma)))).astype(low)
+        grad_up_low = (scaled * silu).astype(low)
+        gated_low = (spread * hidden.astype(full)).astype(low)
+        grad_rows = (
+            matmul(grad_gate_low, gate_all, 1, 1) + matmul(grad_up_low, up_all, 1, 1)
+        ).astype(low)
+        saved.append((grad_gate_low, grad_up_low, gated_low, grad_rows))
+
+    gate_send = jnp.stack(
+        [g.reshape(expert_local, fsdp_size, rows).transpose(1, 0, 2) for g in gate_grads], axis=1
+    )
+    gate_back = lax.all_to_all(gate_send, "fsdp", split_axis=0, concat_axis=0, tiled=True)
+    gate_sum = gate_back[:, 0] + pair_swap(gate_back[:, 1], 2)
+    grad_prob = gate_sum.reshape(experts, rows).T
+
+    grad_rows_own = scatter_plane(saved[0][3])
+    grad_rows_pair = scatter_plane(saved[1][3])
+    grad_from_rows = grad_rows_own.astype(full) + pair_swap(grad_rows_pair, 2).astype(full)
+
+    grad_logits = (
+        probs * (grad_prob - jnp.sum(probs * grad_prob, axis=-1, keepdims=True))
+    ).astype(low)
+    grad_router_t = matmul(grad_logits, ffn_normed, 0, 0)
+    grad_ffn_normed = grad_from_rows + matmul(grad_logits, router_full, 1, 1)
+    grad_scaled = grad_ffn_normed * ffn_gain_f
+    grad_residual = (
+        cotangent
+        + ffn_scale * grad_scaled
+        - residual
+        * (ffn_scale * ffn_scale * ffn_scale)
+        * jnp.mean(residual * grad_scaled, axis=-1, keepdims=True)
+    )
+    grad_ffn_gain_local = jnp.sum(grad_ffn_normed * residual * ffn_scale, axis=0)
+    grad_attn = (row_keep * grad_residual).astype(low)
+    grad_attn_all = line_gather(grad_attn)
+
+    outs = [scatter_plane(matmul(saved[p][2], down_all, 1, 0).astype(low)) for p in range(2)]
+    mixture = outs[0].astype(full) + pair_swap(outs[1], 2).astype(full)
+    block_out = (residual + mixture).astype(low)
+
+    def weight_grad(lefts, rights):
+        total = matmul(lefts[0], rights[0], 0, 0)
+        return total + matmul(lefts[1], rights[1], 0, 0)
+
+    own_cols = expert_local * quarter
+    gates_low = [saved[p][0] for p in range(2)]
+    ups_low = [saved[p][1] for p in range(2)]
+    gated = [saved[p][2] for p in range(2)]
+    grad_gate_own = weight_grad(row_parts, [g[:, :own_cols] for g in gates_low])
+    grad_up_own = weight_grad(row_parts, [g[:, :own_cols] for g in ups_low])
+    grad_down_own = weight_grad([g[:, :own_cols] for g in gated], grad_parts)
+    grad_gate_far = weight_grad(row_parts, [g[:, own_cols:] for g in gates_low]).astype(low)
+    grad_up_far = weight_grad(row_parts, [g[:, own_cols:] for g in ups_low]).astype(low)
+    grad_down_far = weight_grad([g[:, own_cols:] for g in gated], grad_parts).astype(low)
+    grad_gate_sum = grad_gate_own + pair_swap(grad_gate_far, 1).astype(full)
+    grad_up_sum = grad_up_own + pair_swap(grad_up_far, 1).astype(full)
+    grad_down_sum = grad_down_own + pair_swap(grad_down_far, 1).astype(full)
+    grad_w_gate = jnp.stack(
+        [grad_gate_sum[:, e * quarter : (e + 1) * quarter] for e in range(expert_local)], axis=0
+    )
+    grad_w_up = jnp.stack(
+        [grad_up_sum[:, e * quarter : (e + 1) * quarter] for e in range(expert_local)], axis=0
+    )
+    grad_w_down = grad_down_sum.reshape(expert_local, quarter, width)
+
+    grad_mixed = matmul(grad_attn_all, w_out_t, 1, 0).astype(low)
+    grad_output_t = matmul(grad_attn_all, mixed_out, 0, 0)
+    grad_mixed_blocks = grad_mixed.reshape(block_count, block_rows, heads, HD)
+
+    def backward_block(totals, block_in):
+        key_total, value_total = totals
+        query_block, grad_block, log_block = block_in
+        scores = (
+            jnp.einsum("qhd,khd->hqk", query_block, key_heads, preferred_element_type=full)
+            * score_scale
+        )
+        scores = jnp.where(key_valid[None, None, :], scores, -1e30)
+        attn_prob = jnp.exp(scores - log_block[..., None])
+        prob_low = attn_prob.astype(low)
+        value_total = value_total + jnp.einsum(
+            "hqk,qhd->khd", prob_low, grad_block, preferred_element_type=full
+        )
+        grad_prob_block = jnp.einsum(
+            "qhd,khd->hqk", grad_block, value_heads, preferred_element_type=full
+        )
+        row_delta = jnp.sum(attn_prob * grad_prob_block, axis=-1, keepdims=True)
+        grad_scores = (attn_prob * (grad_prob_block - row_delta)).astype(low)
+        grad_query_block = (
+            jnp.einsum("hqk,khd->qhd", grad_scores, key_heads, preferred_element_type=full)
+            * score_scale
+        )
+        key_total = (
+            key_total
+            + jnp.einsum("hqk,qhd->khd", grad_scores, query_block, preferred_element_type=full)
+            * score_scale
+        )
+        return ((key_total, value_total), grad_query_block)
+
+    zero_heads = jnp.zeros((group_rows, heads, HD), full)
+    (grad_key, grad_value), grad_query_blocks = lax.scan(
+        backward_block, (zero_heads, zero_heads), (query_blocks, grad_mixed_blocks, log_totals)
+    )
+    grad_query = grad_query_blocks.reshape(group_rows, heads * HD)
+    prepare_fn = functools.partial(head_prepare, cos_table=cos_table, sin_table=sin_table)
+    grad_query_pre, grad_query_gain_local = jax.vjp(prepare_fn, query_pre, query_gain_f)[1](
+        grad_query
+    )
+    grad_key_pre, grad_key_gain_local = jax.vjp(prepare_fn, key_pre, key_gain_f)[1](
+        grad_key.reshape(group_rows, heads * HD)
+    )
+    grad_qkv = jnp.concatenate(
+        [
+            grad_query_pre.astype(low),
+            grad_key_pre.astype(low),
+            grad_value.reshape(group_rows, heads * HD).astype(low),
+        ],
+        axis=1,
+    )
+    grad_normed_part = matmul(grad_qkv, w_qkv, 1, 1)
+    grad_attn_gain_local = jnp.sum(grad_normed_part * group_full * row_scale, axis=0)
+    grad_normed = line_scatter(
+        [grad_normed_part[k * rows : (k + 1) * rows].astype(low) for k in range(tp_size)]
+    )
+    grad_scaled_in = grad_normed * attn_gain_f
+    own_scale = row_scale[:rows]
+    grad_input = grad_residual + (
+        own_scale * grad_scaled_in
+        - hidden_full
+        * (own_scale * own_scale * own_scale)
+        * jnp.mean(hidden_full * grad_scaled_in, axis=-1, keepdims=True)
+    )
+
+    grad_qkv_w = matmul(group_normed, grad_qkv, 0, 0)
+    weight_pack = jnp.concatenate([grad_qkv_w.astype(low), grad_output_t.astype(low)], axis=1)
+    weight_own = scatter_plane(weight_pack).astype(full)
+    grad_w_query = weight_own[:, :head_width]
+    grad_w_key = weight_own[:, head_width : 2 * head_width]
+    grad_w_value = weight_own[:, 2 * head_width : 3 * head_width]
+    grad_w_output = weight_own[:, 3 * head_width :].T
+
+    both = ("fsdp", "tp")
+    device = fsdp_place * tp_size + tp_place
+    devices = fsdp_size * tp_size
+    piece = width // devices
+    gain_width = query_gain_f.shape[0]
+    head_gains = jnp.zeros((width,), full)
+    head_gains = head_gains.at[:gain_width].set(grad_query_gain_local)
+    head_gains = head_gains.at[gain_width : 2 * gain_width].set(grad_key_gain_local)
+    early = lax.psum(
+        jnp.concatenate([grad_router_t, grad_ffn_gain_local[None, :]], axis=0), both
+    )
+    late = lax.psum(jnp.stack([grad_attn_gain_local, head_gains], axis=0), both)
+    early_own = lax.dynamic_slice_in_dim(early, device * piece, piece, axis=1)
+    grad_router = early_own[:experts].T
+    grad_ffn_gain = early_own[experts]
+    grad_attn_gain = lax.dynamic_slice_in_dim(late[0], device * piece, piece, axis=0)
+    gain_own = gain_width // devices
+    grad_query_gain = lax.dynamic_slice_in_dim(late[1], device * gain_own, gain_own, axis=0)
+    grad_key_gain = lax.dynamic_slice_in_dim(
+        late[1], gain_width + device * gain_own, gain_own, axis=0
+    )
+    return (
+        block_out,
+        grad_input,
+        grad_attn_gain,
+        grad_w_query,
+        grad_w_key,
+        grad_w_value,
+        grad_query_gain,
+        grad_key_gain,
+        grad_w_output,
+        grad_ffn_gain,
+        grad_router,
+        grad_w_gate,
+        grad_w_up,
+        grad_w_down,
+    )
+
+
+def per_device(*arrays):
+    top_count = arrays[3].shape[1]
+    experts = arrays[12].shape[1]
+    if lax.axis_size("tp") == 4 and experts <= 2 * top_count:
+        return per_device_dense(*arrays)
+    return per_device_routed(*arrays)
+
+
 def solution(mesh):
     return jax.shard_map(
         per_device,

time: 2040 us -> 1290 us (0.63)
  waiting for transfers between devices: 1350 us -> 486 us
  matrix products: 278 us -> 398 us
  starting transfers between devices: 21.9 us -> 103 us
  local copies, waits for them, and re-layouts: 157 us -> 79.6 us
  blocking collectives: 82.4 us -> 61 us
    reduce_scatter x9 -> x5, waiting for transfers between devices: 712 us -> 0.03 us  [scatter_plane(): return lax.psum_scatter(values, 'fsdp', scatter_dimension=0, tiled=True)]
    ppermute x0 -> x36, waiting for transfers between devices: none -> 485 us  [the longest x12 305 us: pair_swap(): return lax.ppermute(values, 'tp', [(i, i ^ distance) for i in range(count)])]
    all_gather x9 -> x5, waiting for transfers between devices: 382 us -> 0.04 us  [gather_plane(): return lax.all_gather(values, 'fsdp', axis=0, tiled=True)]
    all_to_all x4 -> x1, waiting for transfers between devices: 224 us -> 0.01 us  [per_device_dense(): lax.all_to_all(gate_send, 'fsdp', split_axis=0, concat_axis=0, tiled=True)]
    dot_general x25 -> x37, matrix products: 247 us -> 375 us  [the longest x35 371 us: matmul(): lax.dot_general(left, right, (((left_dim,), (right_dim,)), ((), ())), pre...]
    ppermute x0 -> x36, starting transfers between devices: none -> 98 us  [the longest x24 79.9 us: shift_tp(): lax.ppermute(values, 'tp', [(i, i + step) for i in range(first, last + 1)])]
    gather x4 -> x0, local copies, waits for them, and re-layouts: 75.6 us -> none  [the longest x1 22.8 us: per_device(): grad_padded[slot_owner]]
    unnamed x2 -> x0, blocking collectives: 54.5 us -> none
  transfers between devices with their start and end apart: 23 -> 48, of which waited for: 19 -> 20; matrix products, arithmetic and copies ran while one was open for 22% -> 44% of each run, Pallas kernels for 0% -> 0%
where the time goes in v1:
time: 1290 us; the launch traced here: 1280 us
  waiting for transfers between devices  486 us (38%)
  matrix products  398 us (31%)
  other arithmetic  138 us (11%)
  starting transfers between devices  103 us (8%)
  local copies, waits for them, and re-layouts  79.6 us (6%)
  blocking collectives  61 us (5%)
  between operations  17.5 us (1%)
    dot_general x35, matrix products, matmul(): lax.dot_general(left, right, (((left_dim,), (right_dim,)), ((), ())), pre...  371 us
    ppermute x12, waiting for transfers between devices, pair_swap(): return lax.ppermute(values, 'tp', [(i, i ^ distance) for i in range(count)])  305 us
    ppermute x24, waiting for transfers between devices, shift_tp(): lax.ppermute(values, 'tp', [(i, i + step) for i in range(first, last + 1)])  180 us
    ppermute x24, starting transfers between devices, shift_tp(): lax.ppermute(values, 'tp', [(i, i + step) for i in range(first, last + 1)])  79.9 us
    psum x1, blocking collectives, per_device_dense(): late = lax.psum(jnp.stack([grad_attn_gain_local, head_gains], axis=0), both)  41.3 us
    unnamed x222, local copies, waits for them, and re-layouts  27.2 us
  transfers between devices with their start and end apart: 48, of which 20 were waited for; matrix products, arithmetic and copies ran while one was open for 44% of the time, Pallas kernels for 0%

profile of v1, /device:TPU:0, one launch (start us, length us, event | category | flops | bytes accessed | tf_op | source)
XLA Modules:
  0.0 1284.0 jit_solution(5026396189565314600)
XLA Ops:
  34.9 5.9 collective-permute-start
  42.2 20.1 %collective-permute-done = bf16[256,2048]{1,0:T(8,128)(2,1)} collective-permute-done((bf16[256,2048]{1,0:T(8,128)(2,1)S(1)}, bf16[256,2048]{1,0:T(8,128)(2,1)}, u32[]{:S(2)}, u32[]{:S(2)}) %collective-permute-start) | collective-permute-done | bytes 1048608 | tf_op jit(solution)/shard_map/ppermute | solution.py:398
  65.1 5.5 collective-permute-start.18
  77.4 40.0 %collective-permute-done.18 = bf16[256,2048]{1,0:T(8,128)(2,1)} collective-permute-done((bf16[256,2048]{1,0:T(8,128)(2,1)}, bf16[256,2048]{1,0:T(8,128)(2,1)}, u32[]{:S(2)}, u32[]{:S(2)}) %collective-permute-start.18) | collective-permute-done | bytes 1048608 | tf_op jit(solution)/shard_map/ppermute | solution.py:394
  121.9 39.5 %collective-permute-done.3 = bf16[256,2048]{1,0:T(8,128)(2,1)S(1)} collective-permute-done((bf16[256,2048]{1,0:T(8,128)(2,1)}, bf16[256,2048]{1,0:T(8,128)(2,1)S(1)}, u32[]{:S(2)}, u32[]{:S(2)}) %collective-permute-start.3) | collective-permute-done | bytes 1048608 | tf_op jit(solution)/shard_map/ppermute | solution.py:398
  163.9 10.4 fusion.55
  211.4 16.4 %while.35 = (s32[]{:T(128)}, bf16[2,512,4,128]{3,2,1,0:T(4,128)(2,1)}, f32[2,4,512]{2,1,0:T(4,128)S(1)}, bf16[2,512,4,128]{3,1,2,0:T(8,128)(2,1)S(1)}, bf16[1024...) while((s32[]{:T(128)}, ...), condition=%wide.region_11.12_spmd.clone, body=%wide.region_8.11_spmd.clone.sunk | while | flops 1099171840 | bytes 37820616 | solution.py:568
  227.9 5.4 convolution_convert_fusion.3
  238.0 18.0 %collective-permute-done.6 = bf16[256,2048]{1,0:T(8,128)(2,1)S(1)} collective-permute-done((bf16[256,2048]{1,0:T(8,128)(2,1)S(1)}, bf16[256,2048]{1,0:T(8,128)(2,1)S(1)}, u32[]{:S(2)}, u32[]{:S(2)}) %collective-permute-start.6) | collective-permute-done | bytes 1048608 | tf_op jit(solution)/shard_map/ppermute | solution.py:398
  261.9 17.2 %collective-permute-done.7 = bf16[256,2048]{1,0:T(8,128)(2,1)S(1)} collective-permute-done((bf16[256,2048]{1,0:T(8,128)(2,1)S(1)}, bf16[256,2048]{1,0:T(8,128)(2,1)S(1)}, u32[]{:S(2)}, u32[]{:S(2)}) %collective-permute-start.7) | collective-permute-done | bytes 1048608 | tf_op jit(solution)/shard_map/ppermute | solution.py:398
  279.8 12.1 collective-permute-start.8
  293.3 18.5 %collective-permute-done.8 = bf16[256,2048]{1,0:T(8,128)(2,1)S(1)} collective-permute-done((bf16[256,2048]{1,0:T(8,128)(2,1)S(1)}, bf16[256,2048]{1,0:T(8,128)(2,1)S(1)}, u32[]{:S(2)}, u32[]{:S(2)}) %collective-permute-start.8) | collective-permute-done | bytes 1048608 | tf_op jit(solution)/shard_map/ppermute | solution.py:398
  319.5 44.8 %collective-permute-done.15 = bf16[256,2048]{1,0:T(8,128)(2,1)S(1)} collective-permute-done((bf16[256,2048]{1,0:T(8,128)(2,1)}, bf16[256,2048]{1,0:T(8,128)(2,1)S(1)}, u32[]{:S(2)}, u32[]{:S(2)}) %collective-permute-start.15) | collective-permute-done | bytes 1048608 | tf_op jit(solution)/shard_map/ppermute | solution.py:394
  378.2 9.5 all_gather.23
  387.7 28.6 %collective-permute-done.16 = bf16[256,16]{0,1:T(8,128)(2,1)S(1)} collective-permute-done((bf16[256,16]{0,1:T(8,128)(2,1)S(1)}, bf16[256,16]{0,1:T(8,128)(2,1)S(1)}, u32[]{:S(2)}, u32[]{:S(2)}) %collective-permute-start.16) | collective-permute-done | bytes 8224 | tf_op jit(solution)/shard_map/ppermute | solution.py:394
  416.3 10.1 all_gather.25
  426.4 15.3 %fusion.154 = f32[1024,2048]{1,0:T(8,128)} fusion(bf16[2048,2048]{1,0:T(8,128)(2,1)} %all-gather.14.cloned.1.call-done, bf16[512,2048]{1,0:T(8,128)(2,1)} %collective-permute-done.14, bf16[512,2048]{1,0:T(8,128)(2,1)} %bitcast.19), kind=kOutput, calls=%fused_computation.350 | convolution fusion | flops 8598323200 | bytes 20971520 | tf_op jit(solution)/shard_map/dot_general | solution.py:438
  441.7 5.7 fusion.175
  447.4 5.8 fusion.174
  454.1 9.7 collective-permute-done.13
  463.8 12.2 fusion.158
  476.0 31.9 %collective-permute-done.12 = bf16[2048,512]{1,0:T(8,128)(2,1)} collective-permute-done((bf16[2048,512]{1,0:T(8,128)(2,1)}, bf16[2048,512]{1,0:T(8,128)(2,1)}, u32[]{:S(2)}, u32[]{:S(2)}) %collective-permute-start.12) | collective-permute-done | bytes 2097184 | tf_op jit(solution)/shard_map/ppermute | solution.py:394
  510.9 22.8 %multiply_convert_fusion.2 = (bf16[2048,1024]{0,1:T(8,128)(2,1)}, bf16[2048,1024]{0,1:T(8,128)(2,1)}, bf16[2048,1024]{0,1:T(8,128)(2,1)}, bf16[2048,1024]{0,1:T(8,128)(2,1)}) fusion(f32[2048,1024]{0,1:T(8,128)} %fusion.158, f32[1024,2048]{1,0:T(8,128)} %fusion.154, f32[2048,256]{0,1:T(8,128)} %broadcast_in_dim.59, f32[2048,256]{0,1:T(8,128)} %broadcast_in_dim.58, ...), kind=kOutput, calls=%fused_computation.75 | convolution fusion | flops 8648654848 | bytes 50331648 | tf_op jit(solution)/shard_map/dot_general | solution.py:438
  533.7 15.2 %fusion.156 = f32[2048,2048]{1,0:T(8,128)} fusion(bf16[2048,1024]{0,1:T(8,128)(2,1)} %get-tuple-element.594, bf16[2048,512]{1,0:T(8,128)(2,1)} %collective-permute-done.13, bf16[2048,256]{1,0:T(8,128)(2,1)S(1)} %get-tuple-element.629, bf16[2048,256]{1,0:T(8,128)(2,1)S(1)} %get-tuple-element.628), kind=kOutput, calls=%fused_computation.352 | convolution fusion | flops 8602517504 | bytes 25165824 | tf_op jit(solution)/shard_map/dot_general | solution.py:438
  548.9 16.5 %add_convert_fusion = bf16[2048,2048]{1,0:T(8,128)(2,1)} fusion(f32[2048,2048]{1,0:T(8,128)} %fusion.156, bf16[2048,1024]{0,1:T(8,128)(2,1)} %get-tuple-element.593, bf16[2048,512]{1,0:T(8,128)(2,1)} %collective-permute-done.12, bf16[2048,256]{1,0:T(8,128)(2,1)S(1)} %copy-done.46, bf16[2048,256]{1,0:T(8,128)(2,1)S(1)} %get-tuple-element.626), kind=kOutput, calls=%fused_computation.53 | convolution fusion | flops 8610906112 | bytes 33554432 | tf_op jit(solution)/shard_map/dot_general | solution.py:438
  565.4 15.6 %convolution_convert_fusion.1 = bf16[2048,2048]{1,0:T(8,128)(2,1)} fusion(bf16[512,2048]{1,0:T(8,128)(2,1)} %collective-permute-done.14, bf16[512,2048]{1,0:T(8,128)(2,1)} %bitcast.19, bf16[2048,1024]{0,1:T(8,128)(2,1)} %get-tuple-element.596, f32[2048,256]{0,1:T(8,128)} %broadcast_in_dim.59, f32[2048,256]{0,1:T(8,128)} %broadcast_in_dim.58), kind=kOutput, calls=%fused_computation.85 | convolution fusion | flops 8615100416 | bytes 20971520 | tf_op jit(solution)/shard_map/dot_general | solution.py:438
  581.1 15.2 %fusion.155 = f32[1024,2048]{1,0:T(8,128)} fusion(bf16[2048,2048]{1,0:T(8,128)(2,1)} %all-gather.12.cloned.1.call-done, bf16[512,2048]{1,0:T(8,128)(2,1)} %collective-permute-done.14, bf16[512,2048]{1,0:T(8,128)(2,1)} %bitcast.19), kind=kOutput, calls=%fused_computation.351 | convolution fusion | flops 8598323200 | bytes 20971520 | tf_op jit(solution)/shard_map/dot_general | solution.py:438
  596.3 14.1 %fusion.159 = f32[2048,1024]{0,1:T(8,128)} fusion(bf16[2048,2048]{1,0:T(8,128)(2,1)} %all-gather.8.cloned.1.call-done, bf16[2048,512]{1,0:T(8,128)(2,1)} %collective-permute-done.13, bf16[2048,256]{1,0:T(8,128)(2,1)S(1)} %get-tuple-element.629, bf16[2048,256]{1,0:T(8,128)(2,1)S(1)} %get-tuple-element.628), kind=kOutput, calls=%fused_computation.355 | convolution fusion | flops 8602517504 | bytes 20971520 | tf_op jit(solution)/shard_map/dot_general | solution.py:438
  613.5 22.9 %multiply_convert_fusion.4 = (bf16[2048,1024]{0,1:T(8,128)(2,1)}, bf16[2048,1024]{0,1:T(8,128)(2,1)}, bf16[2048,1024]{0,1:T(8,128)(2,1)}, bf16[2048,1024]{0,1:T(8,128)(2,1)}) fusion(f32[2048,1024]{0,1:T(8,128)} %fusion.159, f32[1024,2048]{1,0:T(8,128)} %fusion.155, f32[2048,256]{0,1:T(8,128)} %broadcast_in_dim.57, f32[2048,256]{0,1:T(8,128)} %broadcast_in_dim.56, ...), kind=kOutput, calls=%fused_computation.77 | convolution fusion | flops 8648654848 | bytes 50331648 | tf_op jit(solution)/shard_map/dot_general | solution.py:438
  636.4 16.5 %fusion.157 = f32[2048,2048]{1,0:T(8,128)} fusion(bf16[2048,1024]{0,1:T(8,128)(2,1)} %get-tuple-element.590, bf16[2048,512]{1,0:T(8,128)(2,1)} %collective-permute-done.13, bf16[2048,256]{1,0:T(8,128)(2,1)S(1)} %get-tuple-element.629, bf16[2048,256]{1,0:T(8,128)(2,1)S(1)} %get-tuple-element.628), kind=kOutput, calls=%fused_computation.353 | convolution fusion | flops 8602517504 | bytes 25165824 | tf_op jit(solution)/shard_map/dot_general | solution.py:438
  652.9 17.3 %add_convert_fusion.1 = bf16[2048,2048]{1,0:T(8,128)(2,1)} fusion(f32[2048,2048]{1,0:T(8,128)} %fusion.157, bf16[2048,1024]{0,1:T(8,128)(2,1)} %get-tuple-element.589, bf16[2048,512]{1,0:T(8,128)(2,1)} %collective-permute-done.12, bf16[2048,256]{1,0:T(8,128)(2,1)S(1)} %copy-done.47, bf16[2048,256]{1,0:T(8,128)(2,1)S(1)} %get-tuple-element.626), kind=kOutput, calls=%fused_computation.54 | convolution fusion | flops 8610906112 | bytes 33554432 | tf_op jit(solution)/shard_map/dot_general | solution.py:438
  673.0 6.5 convert_multiply_fusion.5
  680.2 6.0 convert_multiply_fusion.3
  691.8 14.8 %convolution_convert_fusion.2 = bf16[2048,2048]{1,0:T(8,128)(2,1)} fusion(bf16[512,2048]{1,0:T(8,128)(2,1)} %collective-permute-done.14, bf16[512,2048]{1,0:T(8,128)(2,1)} %bitcast.19, bf16[2048,1024]{0,1:T(8,128)(2,1)} %get-tuple-element.592, f32[2048,256]{0,1:T(8,128)S(1)} %copy-done.52, f32[2048,256]{0,1:T(8,128)} %broadcast_in_dim.56), kind=kOutput, calls=%fused_computation.86 | convolution fusion | flops 8615100416 | bytes 20971520 | tf_op jit(solution)/shard_map/dot_general | solution.py:438
  706.8 8.3 fusion.77
  715.1 9.4 add_convert_fusion.2
  725.3 9.4 fusion.91
  734.7 8.3 add_convert_fusion.4
  743.9 6.8 fusion.84
  750.6 8.3 add_convert_fusion.3
  763.1 10.7 fusion.95
  773.9 87.9 %collective-permute-done.20 = f32[8,2,256]{2,1,0:T(2,128)S(1)} collective-permute-done((f32[8,2,256]{2,1,0:T(2,128)S(1)}, f32[8,2,256]{2,1,0:T(2,128)S(1)}, u32[]{:S(2)}, u32[]{:S(2)}) %collective-permute-start.20) | collective-permute-done | bytes 16416 | tf_op jit(solution)/shard_map/ppermute | solution.py:394
  865.3 19.1 %collective-permute-done.19 = bf16[256,2048]{1,0:T(8,128)(2,1)} collective-permute-done((bf16[256,2048]{1,0:T(8,128)(2,1)}, bf16[256,2048]{1,0:T(8,128)(2,1)}, u32[]{:S(2)}, u32[]{:S(2)}) %collective-permute-start.19) | collective-permute-done | bytes 1048608 | tf_op jit(solution)/shard_map/ppermute | solution.py:394
  888.1 43.2 %collective-permute-done.17 = bf16[256,2048]{1,0:T(8,128)(2,1)} collective-permute-done((bf16[256,2048]{1,0:T(8,128)(2,1)}, bf16[256,2048]{1,0:T(8,128)(2,1)}, u32[]{:S(2)}, u32[]{:S(2)}) %collective-permute-start.17) | collective-permute-done | bytes 1048608 | tf_op jit(solution)/shard_map/ppermute | solution.py:394
  931.3 6.4 multiply_convert_fusion.7
  939.2 10.8 fusion.88
  954.1 10.7 collective-permute-done.22
  966.2 6.7 fusion.93
  978.0 13.1 %collective-permute-done.23 = bf16[256,2048]{1,0:T(8,128)(2,1)} collective-permute-done((bf16[256,2048]{1,0:T(8,128)(2,1)S(1)}, bf16[256,2048]{1,0:T(8,128)(2,1)}, u32[]{:S(2)}, u32[]{:S(2)}) %collective-permute-start.23) | collective-permute-done | bytes 1048608 | tf_op jit(solution)/shard_map/ppermute | solution.py:398
  992.4 6.7 fusion.86
  1002.4 14.8 %collective-permute-done.24 = bf16[256,2048]{1,0:T(8,128)(2,1)} collective-permute-done((bf16[256,2048]{1,0:T(8,128)(2,1)}, bf16[256,2048]{1,0:T(8,128)(2,1)}, u32[]{:S(2)}, u32[]{:S(2)}) %collective-permute-start.24) | collective-permute-done | bytes 1048608 | tf_op jit(solution)/shard_map/ppermute | solution.py:398
  1022.4 5.1 fusion.110
  1029.8 32.0 %while.36 = (s32[]{:T(128)}, f32[1024,4,128]{0,2,1:T(8,128)S(1)}, f32[1024,4,128]{0,2,1:T(8,128)}, f32[2,512,4,128]{3,1,0,2:T(8,128)}, bf16[2,512,4,128]{3,1,2,0...) while((s32[]{:T(128)}, f32[1024,4,128]{0,2,1:T(8,128)S(1)}, ...), condition=%wide.region_40.41_spmd.clone, body=%wide.region_38.40_spmd.clone.sunk | while | flops 2718697472 | bytes 120650096 | solution.py:721
  1072.1 4.9 multiply_reduce_fusion.3
  1086.3 11.4 convolution_convert_fusion
  1097.6 7.8 pad_maximum_fusion.2
  1105.4 10.7 fusion.81
  1116.1 9.8 fusion.79
  1132.9 14.2 %fusion.48 = (f32[2048]{0:T(1024)S(1)}, bf16[1024,2048]{1,0:T(8,128)(2,1)S(1)}) fusion(f32[1024]{0:T(1024)S(1)} %copy-done.90, bf16[256,2048]{1,0:T(8,128)(2,1)S(1)} %copy-done.40, bf16[256,2048]{1,0:T(8,128)(2,1)S(1)} %copy-done.38, bf16[256,2048]{1,0:T(8,128)(2,1)S(1)} %copy-done.42, bf16[256,2048]{1,0:T(8,128)(2,1)S(1)} %copy-done.17, ...), kind=kOutput, calls=%fused_computation.68 | convolution fusion | flops 6477051904 | bytes 17838080 | tf_op jit(solution)/shard_map/dot_general | solution.py:438
  1152.3 16.4 %collective-permute-done.27 = bf16[256,2048]{1,0:T(8,128)(2,1)S(1)} collective-permute-done((bf16[256,2048]{1,0:T(8,128)(2,1)S(1)}, bf16[256,2048]{1,0:T(8,128)(2,1)S(1)}, u32[]{:S(2)}, u32[]{:S(2)}) %collective-permute-start.27) | collective-permute-done | bytes 1048608 | tf_op jit(solution)/shard_map/ppermute | solution.py:398
  1170.6 5.4 collective-permute-start.28
  1183.0 4.9 convert_add_fusion
  1199.1 22.2 %collective-permute-start.29 = (bf16[256,2048]{1,0:T(8,128)(2,1)}, bf16[256,2048]{1,0:T(8,128)(2,1)}, u32[]{:S(2)}, u32[]{:S(2)}) collective-permute-start(bf16[256,2048]{1,0:T(8,128)(2,1)} %get-tuple-element.609), channel_id=1, source_target_pairs={{0,1},{1,2},{2,3},{4,5},{5,6},{6,7},{8,9},{9,10},{10,11},{12,13},{... | collective-permute-start | bytes 3145736 | tf_op jit(solution)/shard_map/ppermute | solution.py:398
  1222.6 41.3 %psum.14 = f32[2,2048]{1,0:T(2,128)S(1)} all-reduce(f32[2,2048]{1,0:T(2,128)S(1)} %pad_maximum_fusion.20), channel_id=1, replica_groups=mesh['fsdp'=8,'tp'=4] {'fsdp','tp'}, use_global_device_ids=true, to_apply=%region_47.48 | all-reduce | flops 4096 | bytes 32768 | tf_op jit(solution)/shard_map/psum | solution.py:773
  (529 shorter events, 281.4 us)
Async XLA Ops:
  7.2 56.7 %copy-start.24 = (f32[256,2048]{1,0:T(8,128)S(1)}, f32[256,2048]{1,0:T(8,128)}, u32[]{:S(2)}) copy-start(f32[256,2048]{1,0:T(8,128)} %param.51) | copy-start | bytes 6291460
  7.2 155.3 %all-gather.6.cloned.1.call-start = ((), (), s32[]{:S(2)}) async-start(), calls=%async_computation.6 | async-start | bytes 10027008 | tf_op jit(solution)/shard_map/all_gather | solution.py:430
  34.9 391.5 %all-gather.14.cloned.1.call-start = ((), (), s32[]{:S(2)}) async-start(), calls=%async_computation.13 | async-start | bytes 9437184 | tf_op jit(solution)/shard_map/all_gather | solution.py:430
  34.9 27.4 %collective-permute-start = (bf16[256,2048]{1,0:T(8,128)(2,1)S(1)}, bf16[256,2048]{1,0:T(8,128)(2,1)}, u32[]{:S(2)}, u32[]{:S(2)}) collective-permute-start(bf16[256,2048]{1,0:T(8,128)(2,1)S(1)} %copy-done.15), channel_id=1, source_target_pairs={{0,1},{1,2},{2,3},{4,5},{5,6},{6,7},{8,9},{9,10},{10,11},{12,13},{... | collective-permute-start | bytes 3145736 | tf_op jit(solution)/shard_map/ppermute | solution.py:398
  40.9 29.7 %collective-permute-start.1 = (bf16[256,2048]{1,0:T(8,128)(2,1)S(1)}, bf16[256,2048]{1,0:T(8,128)(2,1)}, u32[]{:S(2)}, u32[]{:S(2)}) collective-permute-start(bf16[256,2048]{1,0:T(8,128)(2,1)S(1)} %copy-done.15), channel_id=1, source_target_pairs={{1,0},{2,1},{3,2},{5,4},{6,5},{7,6},{9,8},{10,9},{11,10},{13,12},{... | collective-permute-start | bytes 3145736 | tf_op jit(solution)/shard_map/ppermute | solution.py:398
  62.3 10.2 collective-permute-start.4
  65.1 52.3 %collective-permute-start.18 = (bf16[256,2048]{1,0:T(8,128)(2,1)}, bf16[256,2048]{1,0:T(8,128)(2,1)}, u32[]{:S(2)}, u32[]{:S(2)}) collective-permute-start(bf16[256,2048]{1,0:T(8,128)(2,1)} %convert_element_type.407), channel_id=1, source_target_pairs={{0,2},{1,3},{2,0},{3,1},{4,6},{5,7},{6,4},{7,5},{8,10},{9,11},{10,... | collective-permute-start | bytes 3145736 | tf_op jit(solution)/shard_map/ppermute | solution.py:394
  70.5 46.9 %collective-permute-start.2 = (bf16[256,2048]{1,0:T(8,128)(2,1)}, bf16[256,2048]{1,0:T(8,128)(2,1)}, u32[]{:S(2)}, u32[]{:S(2)}) collective-permute-start(bf16[256,2048]{1,0:T(8,128)(2,1)} %collective-permute-done.1), channel_id=1, source_target_pairs={{1,0},{2,1},{5,4},{6,5},{9,8},{10,9},{13,12},{14,13},{17,16},{18,1... | collective-permute-start | bytes 3145736 | tf_op jit(solution)/shard_map/ppermute | solution.py:398
  72.5 47.6 %collective-permute-start.5 = (bf16[256,2048]{1,0:T(8,128)(2,1)}, bf16[256,2048]{1,0:T(8,128)(2,1)}, u32[]{:S(2)}, u32[]{:S(2)}) collective-permute-start(bf16[256,2048]{1,0:T(8,128)(2,1)} %collective-permute-done.4), channel_id=1, source_target_pairs={{2,3},{6,7},{10,11},{14,15},{18,19},{22,23},{26,27},{30,31}} | collective-permute-start | bytes 3145736 | tf_op jit(solution)/shard_map/ppermute | solution.py:398
  77.3 126.0 %copy-start.29 = (f32[1024,128]{1,0:T(8,128)}, f32[1024,128]{1,0:T(8,128)S(1)}, u32[]{:S(2)}) copy-start(f32[1024,128]{1,0:T(8,128)S(1)} %get-tuple-element.646) | copy-start | bytes 1572868
  77.3 127.2 %copy-start.27 = (f32[1024,128]{1,0:T(8,128)}, f32[1024,128]{1,0:T(8,128)S(1)}, u32[]{:S(2)}) copy-start(f32[1024,128]{1,0:T(8,128)S(1)} %get-tuple-element.645) | copy-start | bytes 1572868
  117.4 324.3 %all-gather.8.cloned.1.call-start = ((), (), s32[]{:S(2)}) async-start(), calls=%async_computation.7 | async-start | bytes 9437184 | tf_op jit(solution)/shard_map/all_gather | solution.py:430
  117.5 43.9 %collective-permute-start.3 = (bf16[256,2048]{1,0:T(8,128)(2,1)}, bf16[256,2048]{1,0:T(8,128)(2,1)S(1)}, u32[]{:S(2)}, u32[]{:S(2)}) collective-permute-start(bf16[256,2048]{1,0:T(8,128)(2,1)} %collective-permute-done.2), channel_id=1, source_target_pairs={{1,0},{5,4},{9,8},{13,12},{17,16},{21,20},{25,24},{29,28}} | collective-permute-start | bytes 3145736 | tf_op jit(solution)/shard_map/ppermute | solution.py:398
  120.1 43.8 %copy-start.37 = (bf16[256,2048]{1,0:T(8,128)(2,1)}, bf16[256,2048]{1,0:T(8,128)(2,1)S(1)}, u32[]{:S(2)}) copy-start(bf16[256,2048]{1,0:T(8,128)(2,1)S(1)} %broadcast_select_fusion.3) | copy-start | bytes 3145732
  163.7 153.7 %copy-start.66 = (f32[1,2048]{1,0:T(1,128)}, f32[1,2048]{1,0:T(1,128)S(1)}, u32[]{:S(2)}) copy-start(f32[1,2048]{1,0:T(1,128)S(1)} %get-tuple-element.642) | copy-start | bytes 24580
  233.4 22.6 %collective-permute-start.6 = (bf16[256,2048]{1,0:T(8,128)(2,1)S(1)}, bf16[256,2048]{1,0:T(8,128)(2,1)S(1)}, u32[]{:S(2)}, u32[]{:S(2)}) collective-permute-start(bf16[256,2048]{1,0:T(8,128)(2,1)S(1)} %get-tuple-element.619), channel_id=1, source_target_pairs={{0,1},{4,5},{8,9},{12,13},{16,17},{20,21},{24,25},{28,29}} | collective-permute-start | bytes 3145736 | tf_op jit(solution)/shard_map/ppermute | solution.py:398
  237.2 18.8 %collective-permute-start.9 = (bf16[256,2048]{1,0:T(8,128)(2,1)S(1)}, bf16[256,2048]{1,0:T(8,128)(2,1)S(1)}, u32[]{:S(2)}, u32[]{:S(2)}) collective-permute-start(bf16[256,2048]{1,0:T(8,128)(2,1)S(1)} %get-tuple-element.620), channel_id=1, source_target_pairs={{3,2},{7,6},{11,10},{15,14},{19,18},{23,22},{27,26},{31,30}} | collective-permute-start | bytes 3145736 | tf_op jit(solution)/shard_map/ppermute | solution.py:398
  256.6 59.4 %copy-start.16 = (bf16[256,2048]{1,0:T(8,128)(2,1)S(1)}, bf16[256,2048]{1,0:T(8,128)(2,1)}, u32[]{:S(2)}) copy-start(bf16[256,2048]{1,0:T(8,128)(2,1)} %param.35) | copy-start | bytes 3145732
  256.6 22.5 %collective-permute-start.7 = (bf16[256,2048]{1,0:T(8,128)(2,1)S(1)}, bf16[256,2048]{1,0:T(8,128)(2,1)S(1)}, u32[]{:S(2)}, u32[]{:S(2)}) collective-permute-start(bf16[256,2048]{1,0:T(8,128)(2,1)S(1)} %get-tuple-element.617), channel_id=1, source_target_pairs={{0,1},{1,2},{4,5},{5,6},{8,9},{9,10},{12,13},{13,14},{16,17},{17,1... | collective-permute-start | bytes 3145736 | tf_op jit(solution)/shard_map/ppermute | solution.py:398
  261.2 17.9 %collective-permute-start.10 = (bf16[256,2048]{1,0:T(8,128)(2,1)S(1)}, bf16[256,2048]{1,0:T(8,128)(2,1)S(1)}, u32[]{:S(2)}, u32[]{:S(2)}) collective-permute-start(bf16[256,2048]{1,0:T(8,128)(2,1)S(1)} %get-tuple-element.618), channel_id=1, source_target_pairs={{2,1},{3,2},{6,5},{7,6},{10,9},{11,10},{14,13},{15,14},{18,17},{19... | collective-permute-start | bytes 3145736 | tf_op jit(solution)/shard_map/ppermute | solution.py:398
  279.8 32.0 %collective-permute-start.8 = (bf16[256,2048]{1,0:T(8,128)(2,1)S(1)}, bf16[256,2048]{1,0:T(8,128)(2,1)S(1)}, u32[]{:S(2)}, u32[]{:S(2)}) collective-permute-start(bf16[256,2048]{1,0:T(8,128)(2,1)S(1)} %get-tuple-element.615), channel_id=1, source_target_pairs={{0,1},{1,2},{2,3},{4,5},{5,6},{6,7},{8,9},{9,10},{10,11},{12,13},{... | collective-permute-start | bytes 3145736 | tf_op jit(solution)/shard_map/ppermute | solution.py:398
  292.0 24.0 %collective-permute-start.11 = (bf16[256,2048]{1,0:T(8,128)(2,1)S(1)}, bf16[256,2048]{1,0:T(8,128)(2,1)S(1)}, u32[]{:S(2)}, u32[]{:S(2)}) collective-permute-start(bf16[256,2048]{1,0:T(8,128)(2,1)S(1)} %get-tuple-element.616), channel_id=1, source_target_pairs={{1,0},{2,1},{3,2},{5,4},{6,5},{7,6},{9,8},{10,9},{11,10},{13,12},{... | collective-permute-start | bytes 3145736 | tf_op jit(solution)/shard_map/ppermute | solution.py:398
  293.3 76.6 %copy-start.80 = (f32[1,256]{1,0:T(1,128)}, f32[1,256]{1,0:T(1,128)S(1)}, u32[]{:S(2)}) copy-start(f32[1,256]{1,0:T(1,128)S(1)} %and_convert_fusion) | copy-start | bytes 3076
  319.4 128.0 %all-gather.10.cloned.1.call-start = ((), (), s32[]{:S(2)}) async-start(), calls=%async_computation.9 | async-start | bytes 9437184 | tf_op jit(solution)/shard_map/all_gather | solution.py:430
  319.4 44.9 %collective-permute-start.15 = (bf16[256,2048]{1,0:T(8,128)(2,1)}, bf16[256,2048]{1,0:T(8,128)(2,1)S(1)}, u32[]{:S(2)}, u32[]{:S(2)}) collective-permute-start(bf16[256,2048]{1,0:T(8,128)(2,1)} %multiply_convert_fusion.8), channel_id=1, source_target_pairs={{0,2},{1,3},{2,0},{3,1},{4,6},{5,7},{6,4},{7,5},{8,10},{9,11},{10,... | collective-permute-start | bytes 3145736 | tf_op jit(solution)/shard_map/ppermute | solution.py:394
  365.3 215.8 %all-gather.12.cloned.1.call-start = ((), (), s32[]{:S(2)}) async-start(), calls=%async_computation.11 | async-start | bytes 9437184 | tf_op jit(solution)/shard_map/all_gather | solution.py:430
  365.9 395.8 %reduce-scatter.12.cloned.1.call-start = ((), (), s32[]{:S(2)}) async-start(), calls=%async_computation.14 | async-start | bytes 9437184 | tf_op jit(solution)/shard_map/reduce_scatter | solution.py:434
  369.9 56.5 %collective-permute-start.14 = (bf16[512,2048]{1,0:T(8,128)(2,1)}, bf16[512,2048]{1,0:T(8,128)(2,1)}, u32[]{:S(2)}, u32[]{:S(2)}) collective-permute-start(bf16[512,2048]{1,0:T(8,128)(2,1)} %bitcast.19), channel_id=1, source_target_pairs={{0,1},{1,0},{2,3},{3,2},{4,5},{5,4},{6,7},{7,6},{8,9},{9,8},{10,11... | collective-permute-start | bytes 6291464 | tf_op jit(solution)/shard_map/ppermute | solution.py:394
  370.0 46.4 %collective-permute-start.16 = (bf16[256,16]{0,1:T(8,128)(2,1)S(1)}, bf16[256,16]{0,1:T(8,128)(2,1)S(1)}, u32[]{:S(2)}, u32[]{:S(2)}) collective-permute-start(bf16[256,16]{0,1:T(8,128)(2,1)S(1)} %multiply_convert_fusion.9), channel_id=1, source_target_pairs={{0,2},{1,3},{2,0},{3,1},{4,6},{5,7},{6,4},{7,5},{8,10},{9,11},{10,... | collective-permute-start | bytes 24584 | tf_op jit(solution)/shard_map/ppermute | solution.py:394
  372.7 91.1 %collective-permute-start.13 = (bf16[2048,512]{1,0:T(8,128)(2,1)}, bf16[2048,512]{1,0:T(8,128)(2,1)}, u32[]{:S(2)}, u32[]{:S(2)}) collective-permute-start(bf16[2048,512]{1,0:T(8,128)(2,1)} %pad_maximum_fusion.12), channel_id=1, source_target_pairs={{0,1},{1,0},{2,3},{3,2},{4,5},{5,4},{6,7},{7,6},{8,9},{9,8},{10,11... | collective-permute-start | bytes 6291464 | tf_op jit(solution)/shard_map/ppermute | solution.py:394
  376.9 131.0 %collective-permute-start.12 = (bf16[2048,512]{1,0:T(8,128)(2,1)}, bf16[2048,512]{1,0:T(8,128)(2,1)}, u32[]{:S(2)}, u32[]{:S(2)}) collective-permute-start(bf16[2048,512]{1,0:T(8,128)(2,1)} %pad_maximum_fusion.11), channel_id=1, source_target_pairs={{0,1},{1,0},{2,3},{3,2},{4,5},{5,4},{6,7},{7,6},{8,9},{9,8},{10,11... | collective-permute-start | bytes 6291464 | tf_op jit(solution)/shard_map/ppermute | solution.py:394
  565.4 296.4 %reduce-scatter.8.cloned.1.call-start = ((), (), s32[]{:S(2)}) async-start(), calls=%async_computation.10 | async-start | bytes 9437184 | tf_op jit(solution)/shard_map/reduce_scatter | solution.py:434
  581.0 284.3 %reduce-scatter.10.cloned.1.call-start = ((), (), s32[]{:S(2)}) async-start(), calls=%async_computation.12 | async-start | bytes 9437184 | tf_op jit(solution)/shard_map/reduce_scatter | solution.py:434
  687.6 72.5 %all-to-all-start = ((f32[8,2,2,256]{3,2,1,0:T(2,128)}), f32[8,2,2,256]{3,2,1,0:T(2,128)S(1)}, u32[]{:S(2)}, u32[]{:S(2)}) async-start(f32[8,2,2,256]{3,2,1,0:T(2,128)} %pad_maximum_fusion.19), calls=%async_computation.4 | async-start | bytes 65536 | tf_op jit(solution)/shard_map/all_to_all | solution.py:633
  691.8 196.3 %reduce-scatter.6.cloned.1.call-start = ((), (), s32[]{:S(2)}) async-start(), calls=%async_computation.8 | async-start | bytes 9437184 | tf_op jit(solution)/shard_map/reduce_scatter | solution.py:434
  706.7 481.2 %all-reduce.8.cloned.1.call-start = ((), (), s32[]{:S(2)}) async-start(), calls=%async_computation.16 | async-start | bytes 393216 | tf_op jit(solution)/shard_map/psum | solution.py:770
  724.5 455.9 %collective-permute-start.35 = (bf16[512,2048]{1,0:T(8,128)(2,1)}, bf16[512,2048]{1,0:T(8,128)(2,1)}, u32[]{:S(2)}, u32[]{:S(2)}) collective-permute-start(bf16[512,2048]{1,0:T(8,128)(2,1)} %add_convert_fusion.2), channel_id=1, source_target_pairs={{0,1},{1,0},{2,3},{3,2},{4,5},{5,4},{6,7},{7,6},{8,9},{9,8},{10,11... | collective-permute-start | bytes 6291464 | tf_op jit(solution)/shard_map/ppermute | solution.py:394
  743.0 383.0 %collective-permute-start.33 = (bf16[2048,512]{1,0:T(8,128)(2,1)}, bf16[2048,512]{1,0:T(8,128)(2,1)}, u32[]{:S(2)}, u32[]{:S(2)}) collective-permute-start(bf16[2048,512]{1,0:T(8,128)(2,1)} %add_convert_fusion.4), channel_id=1, source_target_pairs={{0,1},{1,0},{2,3},{3,2},{4,5},{5,4},{6,7},{7,6},{8,9},{9,8},{10,11... | collective-permute-start | bytes 6291464 | tf_op jit(solution)/shard_map/ppermute | solution.py:394
  759.0 370.0 %collective-permute-start.34 = (bf16[2048,512]{1,0:T(8,128)(2,1)}, bf16[2048,512]{1,0:T(8,128)(2,1)}, u32[]{:S(2)}, u32[]{:S(2)}) collective-permute-start(bf16[2048,512]{1,0:T(8,128)(2,1)} %add_convert_fusion.3), channel_id=1, source_target_pairs={{0,1},{1,0},{2,3},{3,2},{4,5},{5,4},{6,7},{7,6},{8,9},{9,8},{10,11... | collective-permute-start | bytes 6291464 | tf_op jit(solution)/shard_map/ppermute | solution.py:394
  760.1 124.3 %copy-start.8 = (f32[256,2048]{1,0:T(8,128)S(1)}, f32[256,2048]{1,0:T(8,128)}, u32[]{:S(2)}) copy-start(f32[256,2048]{1,0:T(8,128)} %copy-done.7) | copy-start | bytes 6291460
  760.1 124.3 %copy-start.67 = (f32[1,2048]{1,0:T(1,128)S(1)}, f32[1,2048]{1,0:T(1,128)}, u32[]{:S(2)}) copy-start(f32[1,2048]{1,0:T(1,128)} %copy-done.66) | copy-start | bytes 24580
  760.1 124.3 %copy-start.79 = (f32[256]{0:T(256)S(1)}, f32[256]{0:T(256)}, u32[]{:S(2)}) copy-start(f32[256]{0:T(256)} %copy-done.78) | copy-start | bytes 3076
  760.1 101.7 %collective-permute-start.20 = (f32[8,2,256]{2,1,0:T(2,128)S(1)}, f32[8,2,256]{2,1,0:T(2,128)S(1)}, u32[]{:S(2)}, u32[]{:S(2)}) collective-permute-start(f32[8,2,256]{2,1,0:T(2,128)S(1)} %slice_bitcast_fusion.10), channel_id=1, source_target_pairs={{0,2},{1,3},{2,0},{3,1},{4,6},{5,7},{6,4},{7,5},{8,10},{9,11},{10,... | collective-permute-start | bytes 49160 | tf_op jit(solution)/shard_map/ppermute | solution.py:394
  761.6 122.8 %collective-permute-start.19 = (bf16[256,2048]{1,0:T(8,128)(2,1)}, bf16[256,2048]{1,0:T(8,128)(2,1)}, u32[]{:S(2)}, u32[]{:S(2)}) collective-permute-start(bf16[256,2048]{1,0:T(8,128)(2,1)} %reduce-scatter.12.cloned.1.call-done), channel_id=1, source_target_pairs={{0,2},{1,3},{2,0},{3,1},{4,6},{5,7},{6,4},{7,5},{8,10},{9,11},{10,... | collective-permute-start | bytes 3145736 | tf_op jit(solution)/shard_map/ppermute | solution.py:394
  773.8 157.4 %copy-start.81 = (f32[1,256]{1,0:T(1,128)S(1)}, f32[1,256]{1,0:T(1,128)}, u32[]{:S(2)}) copy-start(f32[1,256]{1,0:T(1,128)} %copy-done.80) | copy-start | bytes 3076
  773.9 157.4 %copy-start.92 = (f32[256]{0:T(256)S(1)}, f32[256]{0:T(256)}, u32[]{:S(2)}) copy-start(f32[256]{0:T(256)} %get-tuple-element.652) | copy-start | bytes 3076
  861.8 69.5 %collective-permute-start.17 = (bf16[256,2048]{1,0:T(8,128)(2,1)}, bf16[256,2048]{1,0:T(8,128)(2,1)}, u32[]{:S(2)}, u32[]{:S(2)}) collective-permute-start(bf16[256,2048]{1,0:T(8,128)(2,1)} %reduce-scatter.8.cloned.1.call-done), channel_id=1, source_target_pairs={{0,2},{1,3},{2,0},{3,1},{4,6},{5,7},{6,4},{7,5},{8,10},{9,11},{10,... | collective-permute-start | bytes 3145736 | tf_op jit(solution)/shard_map/ppermute | solution.py:394
  937.6 27.2 %collective-permute-start.22 = (bf16[256,2048]{1,0:T(8,128)(2,1)S(1)}, bf16[256,2048]{1,0:T(8,128)(2,1)S(1)}, u32[]{:S(2)}, u32[]{:S(2)}) collective-permute-start(bf16[256,2048]{1,0:T(8,128)(2,1)S(1)} %get-tuple-element.581), channel_id=1, source_target_pairs={{1,0},{2,1},{3,2},{5,4},{6,5},{7,6},{9,8},{10,9},{11,10},{13,12},{... | collective-permute-start | bytes 3145736 | tf_op jit(solution)/shard_map/ppermute | solution.py:398
  950.0 42.4 %copy-start.99 = (bf16[2048,1024]{0,1:T(8,128)(2,1)S(1)}, bf16[2048,1024]{0,1:T(8,128)(2,1)}, u32[]{:S(2)}) copy-start(bf16[2048,1024]{0,1:T(8,128)(2,1)} %get-tuple-element.594) | copy-start | bytes 12582916
  950.0 26.3 %collective-permute-start.21 = (bf16[256,2048]{1,0:T(8,128)(2,1)S(1)}, bf16[256,2048]{1,0:T(8,128)(2,1)S(1)}, u32[]{:S(2)}, u32[]{:S(2)}) collective-permute-start(bf16[256,2048]{1,0:T(8,128)(2,1)S(1)} %get-tuple-element.581), channel_id=1, source_target_pairs={{0,1},{1,2},{2,3},{4,5},{5,6},{6,7},{8,9},{9,10},{10,11},{12,13},{... | collective-permute-start | bytes 3145736 | tf_op jit(solution)/shard_map/ppermute | solution.py:398
  964.9 26.2 %collective-permute-start.23 = (bf16[256,2048]{1,0:T(8,128)(2,1)S(1)}, bf16[256,2048]{1,0:T(8,128)(2,1)}, u32[]{:S(2)}, u32[]{:S(2)}) collective-permute-start(bf16[256,2048]{1,0:T(8,128)(2,1)S(1)} %collective-permute-done.22), channel_id=1, source_target_pairs={{1,0},{2,1},{5,4},{6,5},{9,8},{10,9},{13,12},{14,13},{17,16},{18,1... | collective-permute-start | bytes 3145736 | tf_op jit(solution)/shard_map/ppermute | solution.py:398
  976.4 23.8 %collective-permute-start.25 = (bf16[256,2048]{1,0:T(8,128)(2,1)S(1)}, bf16[256,2048]{1,0:T(8,128)(2,1)}, u32[]{:S(2)}, u32[]{:S(2)}) collective-permute-start(bf16[256,2048]{1,0:T(8,128)(2,1)S(1)} %collective-permute-done.21), channel_id=1, source_target_pairs={{1,2},{2,3},{5,6},{6,7},{9,10},{10,11},{13,14},{14,15},{17,18},{18... | collective-permute-start | bytes 3145736 | tf_op jit(solution)/shard_map/ppermute | solution.py:398
  991.1 26.1 %collective-permute-start.24 = (bf16[256,2048]{1,0:T(8,128)(2,1)}, bf16[256,2048]{1,0:T(8,128)(2,1)}, u32[]{:S(2)}, u32[]{:S(2)}) collective-permute-start(bf16[256,2048]{1,0:T(8,128)(2,1)} %collective-permute-done.23), channel_id=1, source_target_pairs={{1,0},{5,4},{9,8},{13,12},{17,16},{21,20},{25,24},{29,28}} | collective-permute-start | bytes 3145736 | tf_op jit(solution)/shard_map/ppermute | solution.py:398
  1000.1 271.7 %reduce-scatter.14.cloned.1.call-start = ((), (), s32[]{:S(2)}) async-start(), calls=%async_computation.15 | async-start | bytes 9437184 | tf_op jit(solution)/shard_map/reduce_scatter | solution.py:434
  1000.1 18.4 %collective-permute-start.26 = (bf16[256,2048]{1,0:T(8,128)(2,1)}, bf16[256,2048]{1,0:T(8,128)(2,1)S(1)}, u32[]{:S(2)}, u32[]{:S(2)}) collective-permute-start(bf16[256,2048]{1,0:T(8,128)(2,1)} %collective-permute-done.25), channel_id=1, source_target_pairs={{2,3},{6,7},{10,11},{14,15},{18,19},{22,23},{26,27},{30,31}} | collective-permute-start | bytes 3145736 | tf_op jit(solution)/shard_map/ppermute | solution.py:398
  1147.3 21.4 %collective-permute-start.27 = (bf16[256,2048]{1,0:T(8,128)(2,1)S(1)}, bf16[256,2048]{1,0:T(8,128)(2,1)S(1)}, u32[]{:S(2)}, u32[]{:S(2)}) collective-permute-start(bf16[256,2048]{1,0:T(8,128)(2,1)S(1)} %get-tuple-element.613), channel_id=1, source_target_pairs={{0,1},{4,5},{8,9},{12,13},{16,17},{20,21},{24,25},{28,29}} | collective-permute-start | bytes 3145736 | tf_op jit(solution)/shard_map/ppermute | solution.py:398
  1148.7 20.0 %collective-permute-start.30 = (bf16[256,2048]{1,0:T(8,128)(2,1)S(1)}, bf16[256,2048]{1,0:T(8,128)(2,1)S(1)}, u32[]{:S(2)}, u32[]{:S(2)}) collective-permute-start(bf16[256,2048]{1,0:T(8,128)(2,1)S(1)} %get-tuple-element.614), channel_id=1, source_target_pairs={{3,2},{7,6},{11,10},{15,14},{19,18},{23,22},{27,26},{31,30}} | collective-permute-start | bytes 3145736 | tf_op jit(solution)/shard_map/ppermute | solution.py:398
  1170.6 24.0 %collective-permute-start.28 = (bf16[256,2048]{1,0:T(8,128)(2,1)}, bf16[256,2048]{1,0:T(8,128)(2,1)}, u32[]{:S(2)}, u32[]{:S(2)}) collective-permute-start(bf16[256,2048]{1,0:T(8,128)(2,1)} %get-tuple-element.611), channel_id=1, source_target_pairs={{0,1},{1,2},{4,5},{5,6},{8,9},{9,10},{12,13},{13,14},{16,17},{17,1... | collective-permute-start | bytes 3145736 | tf_op jit(solution)/shard_map/ppermute | solution.py:398
  1176.1 18.6 %collective-permute-start.31 = (bf16[256,2048]{1,0:T(8,128)(2,1)}, bf16[256,2048]{1,0:T(8,128)(2,1)}, u32[]{:S(2)}, u32[]{:S(2)}) collective-permute-start(bf16[256,2048]{1,0:T(8,128)(2,1)} %get-tuple-element.612), channel_id=1, source_target_pairs={{2,1},{3,2},{6,5},{7,6},{10,9},{11,10},{14,13},{15,14},{18,17},{19... | collective-permute-start | bytes 3145736 | tf_op jit(solution)/shard_map/ppermute | solution.py:398
  1190.6 77.1 %copy-start.25 = (f32[256,2048]{1,0:T(8,128)S(1)}, f32[256,2048]{1,0:T(8,128)}, u32[]{:S(2)}) copy-start(f32[256,2048]{1,0:T(8,128)} %get-tuple-element.582) | copy-start | bytes 6291460
  1190.6 77.2 %copy-start.87 = (f32[256]{0:T(256)S(1)}, f32[256]{0:T(256)}, u32[]{:S(2)}) copy-start(f32[256]{0:T(256)} %copy-done.86) | copy-start | bytes 3076
  1190.6 77.2 %copy-start.91 = (f32[256,1]{0,1:T(1,128)S(1)}, f32[256,1]{0,1:T(1,128)}, u32[]{:S(2)}) copy-start(f32[256,1]{0,1:T(1,128)} %multiply_multiply_fusion.2) | copy-start | bytes 3076
  1199.1 66.1 %collective-permute-start.29 = (bf16[256,2048]{1,0:T(8,128)(2,1)}, bf16[256,2048]{1,0:T(8,128)(2,1)}, u32[]{:S(2)}, u32[]{:S(2)}) collective-permute-start(bf16[256,2048]{1,0:T(8,128)(2,1)} %get-tuple-element.609), channel_id=1, source_target_pairs={{0,1},{1,2},{2,3},{4,5},{5,6},{6,7},{8,9},{9,10},{10,11},{12,13},{... | collective-permute-start | bytes 3145736 | tf_op jit(solution)/shard_map/ppermute | solution.py:398
  1221.3 43.9 %collective-permute-start.32 = (bf16[256,2048]{1,0:T(8,128)(2,1)}, bf16[256,2048]{1,0:T(8,128)(2,1)}, u32[]{:S(2)}, u32[]{:S(2)}) collective-permute-start(bf16[256,2048]{1,0:T(8,128)(2,1)} %get-tuple-element.610), channel_id=1, source_target_pairs={{1,0},{2,1},{3,2},{5,4},{6,5},{7,6},{9,8},{10,9},{11,10},{13,12},{... | collective-permute-start | bytes 3145736 | tf_op jit(solution)/shard_map/ppermute | solution.py:398
  (104 other events, 787.1 us)
Sparse Core Ops, SparseCore 0:
  35.0 60.9 all-gather.5
  117.5 72.6 all-gather.13
  319.5 52.9 all-gather.7
  374.9 54.4 all-gather.9
  431.1 54.2 all-gather.11
  565.5 70.4 reduce-scatter.11
  639.4 71.4 reduce-scatter.7
  714.4 71.4 reduce-scatter.9
  789.4 71.4 reduce-scatter.5
  1000.2 126.0 all-reduce.7
  1129.8 72.2 reduce-scatter.13
